TPU v7x, 512 devices: a whole 4x8x8 slice. The times are simulated.
512 devices in a mesh: ctx: 64 (over y, x, z_lo), fsdp: 8 (over z_hi, core).
Axes of the slice: x: 4, y: 8, z: 8 (z_hi: 4, z_lo: 2; z = z_hi * 2 + z_lo), core: 2. Of those that a mesh axis runs over, the one named last changes fastest.
Arguments:
- rotated_query_rows: bfloat16 [12288, 4096], P('ctx', 'fsdp'), may hold values from -6 to 6
- rotated_key_rows: bfloat16 [12288, 4096], P('ctx', 'fsdp'), may hold values from -6 to 6
- saved_value_rows: bfloat16 [12288, 4096], P('ctx', 'fsdp'), may hold values from -6 to 6
- projection_output_gradient: bfloat16 [12288, 5120], P('ctx', 'fsdp'), may hold values from -6 to 6
- frozen_weight_codes: int32 [5120, 4096], P('ctx', 'fsdp'), may hold values from 0 to 15
- block_scale_index: int32 [5120, 64], P('ctx', 'fsdp'), may hold values from 0 to 255
- block_scale_table: float32 [256], replicated, may hold values from 0.008385255 to 0.08385255
- adapter_down_matrix: bfloat16 [64, 4096], P('ctx', 'fsdp'), may hold values from -0.75 to 0.75
- adapter_up_matrix: bfloat16 [64, 5120], P('ctx', 'fsdp'), may hold values from -0.078125 to 0.078125
Outputs:
- query_grad: bfloat16 [12288, 4096], P('ctx', 'fsdp')
- key_grad: bfloat16 [12288, 4096], P('ctx', 'fsdp')
- value_grad: bfloat16 [12288, 4096], P('ctx', 'fsdp')
- down_matrix_gradient: float32 [64, 4096], P('ctx', 'fsdp')
- up_matrix_gradient: float32 [64, 5120], P('ctx', 'fsdp')
All inputs are finite; a program needn't handle non-finite values.
Results may differ from a plain program's by a relative error of at most 0.0093.
Values may be sent and summed in bfloat16 or wider, within the bound.
A program may use at most 64 MiB of HBM per device.

v0:
```python
import jax
import jax.numpy as jnp
from jax import lax
from jax.sharding import PartitionSpec as P

HEAD_WIDTH = 128
GROUP_DEV = 8


nf4_values = (
    -1.0,
    -0.6961928009986877,
    -0.5250730514526367,
    -0.39491748809814453,
    -0.28444138169288635,
    -0.18477343022823334,
    -0.09105003625154495,
    0.0,
    0.07958029955625534,
    0.16093020141124725,
    0.24611230194568634,
    0.33791524171829224,
    0.44070982933044434,
    0.5626170039176941,
    0.7229568362236023,
    1.0,
)
adapter_scale = 0.25
masked = -1e30


def in_order(pieces, dim):
    shape = list(pieces.shape[1:])
    shape[dim] *= pieces.shape[0]
    return jnp.moveaxis(pieces, 0, dim).reshape(shape)


def copy_for_each(x, axis):
    copies = jnp.broadcast_to(x, (lax.axis_size(axis), *x.shape))
    return lax.all_to_all(copies, axis, split_axis=0, concat_axis=0, tiled=True)


def gather_directly(x, axis, dim):
    return in_order(copy_for_each(x, axis), dim)


def side_by_side(arrays, axis, dim, along):
    widths = [a.shape[along] for a in arrays]
    both = jnp.concatenate(arrays, axis=along)
    result = lax.all_gather(both, axis, axis=dim, tiled=True)
    return tuple(jnp.split(result, [sum(widths[:k]) for k in range(1, len(widths))], axis=along))


def passed_along(block, axis, distance):
    devices = range(lax.axis_size(axis))
    route = [((i - distance) % len(devices), i) for i in devices]
    return lax.ppermute(block, axis, route)


def of_everyone(x, axis):
    return copy_for_each(x, axis).sum(axis=0)


def in_blocks(x, dim, peers):
    shape = x.shape
    pieces = x.reshape(*shape[:dim], peers, shape[dim] // peers, *shape[dim + 1 :])
    return jnp.moveaxis(pieces, dim, 0)


def sum_at_owner(x, axis, dim):
    peers = lax.axis_size(axis)
    pieces = lax.all_to_all(in_blocks(x, dim, peers), axis, 0, 0, tiled=True)
    return jnp.sum(pieces, axis=0)


def in_one_piece(arrays, axis, dim, along):
    widths = [a.shape[along] for a in arrays]
    both = jnp.concatenate(arrays, axis=along)
    result = sum_at_owner(both, axis, dim)
    return tuple(jnp.split(result, [sum(widths[:k]) for k in range(1, len(widths))], axis=along))


def dequantize(frozen_weight_codes, block_scale_index, block_scale_table):
    values = jnp.zeros(frozen_weight_codes.shape, jnp.float32)
    for level_code in range(16):
        values = values + jnp.where(frozen_weight_codes == level_code, nf4_values[level_code], 0.0)
    level_iota = lax.broadcasted_iota(jnp.int32, (1, 1, block_scale_table.shape[0]), 2)
    picked = jnp.sum(
        jnp.where(block_scale_index[:, :, None] == level_iota, block_scale_table, 0.0), axis=-1
    )
    scales = jnp.repeat(picked, frozen_weight_codes.shape[1] // block_scale_index.shape[1], axis=1)
    return (values * scales).astype(jnp.bfloat16)


def on_device(
    rotated_query_rows,
    rotated_key_rows,
    saved_value_rows,
    projection_output_gradient,
    frozen_weight_codes,
    block_scale_index,
    block_scale_table,
    adapter_down_matrix,
    adapter_up_matrix,
):
    tok_rows = rotated_query_rows.shape[0]
    head_count = rotated_query_rows.shape[1] // HEAD_WIDTH
    group_dev = GROUP_DEV
    score_scale = HEAD_WIDTH ** (-0.5)
    ctx_index = lax.axis_index("ctx")
    weight_local = dequantize(frozen_weight_codes, block_scale_index, block_scale_table)
    full_grad = gather_directly(projection_output_gradient, "fsdp", 1)
    down_projected_full, up_rows = side_by_side(
        (adapter_down_matrix, adapter_up_matrix), "ctx", 0, 1
    )
    backward_piece = jnp.einsum(
        "td,rd->tr", projection_output_gradient, up_rows, preferred_element_type=jnp.float32
    )
    adapter_backward = (adapter_scale * lax.psum(backward_piece, "fsdp")).astype(jnp.bfloat16)
    frozen_input_gradient = jnp.dot(
        full_grad,
        lax.all_gather(weight_local, "ctx", axis=0, tiled=True),
        preferred_element_type=jnp.float32,
    )
    attention_gradient = (
        frozen_input_gradient
        + jnp.dot(adapter_backward, down_projected_full, preferred_element_type=jnp.float32)
    ).astype(jnp.bfloat16)
    arrived = [
        passed_along((rotated_key_rows, saved_value_rows), "ctx", offset)
        for offset in range(1, group_dev)
    ]
    head_shape = (tok_rows, head_count, HEAD_WIDTH)
    query_major = rotated_query_rows.reshape(head_shape).transpose(1, 0, 2)
    key_major = rotated_key_rows.reshape(head_shape).transpose(1, 0, 2)
    value_major = saved_value_rows.reshape(head_shape).transpose(1, 0, 2)
    grad_major = attention_gradient.reshape(head_shape).transpose(1, 0, 2)
    keys_major = (
        jnp.concatenate([rotated_key_rows] + [shifted_pair[0] for shifted_pair in arrived], 0)
        .reshape(-1, head_count, HEAD_WIDTH)
        .transpose(1, 0, 2)
    )
    values_major = (
        jnp.concatenate([saved_value_rows] + [shifted_pair[1] for shifted_pair in arrived], 0)
        .reshape(-1, head_count, HEAD_WIDTH)
        .transpose(1, 0, 2)
    )
    key_span = group_dev * tok_rows
    row_iota = lax.broadcasted_iota(jnp.int32, (tok_rows, key_span), 0)
    col_iota = lax.broadcasted_iota(jnp.int32, (tok_rows, key_span), 1)
    col_block = col_iota // tok_rows
    causal = (col_block > 0) | (col_iota <= row_iota)
    plain_ok = causal & (col_block <= ctx_index % group_dev)
    shift_ok = causal & (col_block <= (ctx_index + group_dev // 2) % group_dev)
    plain_flags = jnp.arange(head_count) < head_count // 2

    def attend_head(inputs):
        query_one, keys_one, values_one, grad_one, is_plain = inputs
        allowed = jnp.where(is_plain, plain_ok, shift_ok)
        scores = jnp.dot(query_one, keys_one.T, preferred_element_type=jnp.float32) * score_scale
        scores = jnp.where(allowed, scores, masked)
        row_max = jnp.max(scores, axis=-1, keepdims=True)
        row_sum = jnp.sum(jnp.exp(scores - row_max), axis=-1, keepdims=True)
        log_norm = row_max + jnp.log(row_sum)
        prob_full = jnp.exp(scores - log_norm)
        prob_half = prob_full.astype(jnp.bfloat16)
        attn_one = jnp.dot(prob_half, values_one, preferred_element_type=jnp.float32).astype(
            jnp.bfloat16
        )
        prob_grad = jnp.dot(grad_one, values_one.T, preferred_element_type=jnp.float32)
        row_delta = jnp.sum(prob_full * prob_grad, axis=-1, keepdims=True)
        score_grad = (prob_full * (prob_grad - row_delta) * score_scale).astype(jnp.bfloat16)
        query_one_grad = jnp.dot(score_grad, keys_one, preferred_element_type=jnp.float32)
        key_one_part = jnp.dot(
            score_grad[:, :tok_rows].T, query_one, preferred_element_type=jnp.float32
        )
        value_one_part = jnp.dot(
            prob_half[:, :tok_rows].T, grad_one, preferred_element_type=jnp.float32
        )
        return (
            attn_one,
            query_one_grad,
            key_one_part,
            value_one_part,
            log_norm[:, 0],
            row_delta[:, 0],
        )

    attn_major, query_grad_major, key_major_part, value_major_part, norm_major, delta_major = (
        lax.map(attend_head, (query_major, keys_major, values_major, grad_major, plain_flags))
    )
    attention_output = attn_major.transpose(1, 0, 2)
    query_grad = query_grad_major.transpose(1, 0, 2)
    rows_out = [
        passed_along((rotated_query_rows, attention_gradient), "ctx", -offset)
        for offset in range(1, group_dev)
    ]
    stats_out = [
        passed_along((norm_major, delta_major), "ctx", -offset) for offset in range(1, group_dev)
    ]
    far_query = (
        jnp.concatenate([shifted_pair[0] for shifted_pair in rows_out], 0)
        .reshape(-1, head_count, HEAD_WIDTH)
        .transpose(1, 0, 2)
    )
    far_grad = (
        jnp.concatenate([shifted_pair[1] for shifted_pair in rows_out], 0)
        .reshape(-1, head_count, HEAD_WIDTH)
        .transpose(1, 0, 2)
    )
    far_norm = jnp.concatenate([shifted_pair[0] for shifted_pair in stats_out], 1)
    far_delta = jnp.concatenate([shifted_pair[1] for shifted_pair in stats_out], 1)
    far_rows = lax.broadcasted_iota(jnp.int32, ((group_dev - 1) * tok_rows, 1), 0)
    row_offset = far_rows // tok_rows + 1
    far_plain = row_offset <= (ctx_index + row_offset) % group_dev
    far_shift = row_offset <= (ctx_index + row_offset + group_dev // 2) % group_dev

    def far_head(inputs):
        query_far, grad_far, key_one, value_one, norm_far, delta_far, is_plain = inputs
        allowed_far = jnp.where(is_plain, far_plain, far_shift)
        far_scores = jnp.dot(query_far, key_one.T, preferred_element_type=jnp.float32) * score_scale
        far_scores = jnp.where(allowed_far, far_scores, masked)
        far_prob = jnp.exp(far_scores - norm_far[:, None])
        far_prob_grad = jnp.dot(grad_far, value_one.T, preferred_element_type=jnp.float32)
        far_score_grad = (far_prob * (far_prob_grad - delta_far[:, None]) * score_scale).astype(
            jnp.bfloat16
        )
        key_far = jnp.dot(far_score_grad.T, query_far, preferred_element_type=jnp.float32)
        value_far = jnp.dot(
            far_prob.astype(jnp.bfloat16).T, grad_far, preferred_element_type=jnp.float32
        )
        return (key_far, value_far)

    key_far_major, value_far_major = lax.map(
        far_head, (far_query, far_grad, key_major, value_major, far_norm, far_delta, plain_flags)
    )
    key_grad = (key_major_part + key_far_major).transpose(1, 0, 2)
    value_grad = (value_major_part + value_far_major).transpose(1, 0, 2)
    attention_flat = attention_output.reshape(tok_rows, -1)
    middle_piece = jnp.einsum(
        "te,re->tr", attention_flat, down_projected_full, preferred_element_type=jnp.float32
    )
    adapter_middle = of_everyone(middle_piece, "fsdp").astype(jnp.bfloat16)
    up_piece = adapter_scale * jnp.einsum(
        "vu,vp->up", adapter_middle, projection_output_gradient, preferred_element_type=jnp.float32
    )
    down_piece = jnp.einsum(
        "mq,ms->qs", adapter_backward, attention_flat, preferred_element_type=jnp.float32
    )
    up_matrix_gradient, down_matrix_gradient = in_one_piece((up_piece, down_piece), "ctx", 0, 1)
    return (
        query_grad.reshape(tok_rows, -1).astype(jnp.bfloat16),
        key_grad.reshape(tok_rows, -1).astype(jnp.bfloat16),
        value_grad.reshape(tok_rows, -1).astype(jnp.bfloat16),
        down_matrix_gradient,
        up_matrix_gradient,
    )


def solution(mesh):
    in_specs = (
        P("ctx", "fsdp"),
        P("ctx", "fsdp"),
        P("ctx", "fsdp"),
        P("ctx", "fsdp"),
        P("ctx", "fsdp"),
        P("ctx", "fsdp"),
        P(),
        P("ctx", "fsdp"),
        P("ctx", "fsdp"),
    )
    out_specs = (
        P("ctx", "fsdp"),
        P("ctx", "fsdp"),
        P("ctx", "fsdp"),
        P("ctx", "fsdp"),
        P("ctx", "fsdp"),
    )
    return jax.shard_map(
        on_device, mesh=mesh, in_specs=in_specs, out_specs=out_specs, check_vma=False
    )
```

profile of v0, /device:TPU:1, one launch (start us, length us, event | category | flops | bytes accessed | tf_op | source)
XLA Modules:
  0.0 576.3 jit_solution(11243099354768312076)
XLA Ops:
  12.6 11.9 %all-to-all-start = ((bf16[8,192,640]{2,1,0:T(8,128)(2,1)}), bf16[8,192,640]{2,1,0:T(8,128)(2,1)}, u32[]{:S(2)}, u32[]{:S(2)}) async-start(bf16[8,192,640]{2,1,0:T(8,128)(2,1)} %broadcast_in_dim.153), calls=%async_computation | async-start | bytes 3932160 | tf_op jit(solution)/shard_map/all_to_all | solution.py:40
  24.7 4.7 collective-permute-start.10
  29.4 4.1 collective-permute-start.11
  33.4 4.4 collective-permute-start.12
  40.4 3.7 collective-permute-start.7
  44.2 185.3 %all-gather = bf16[64,1,1152]{2,1,0:T(2,128)(2,1)S(1)} all-gather(bf16[1,1,1152]{2,1,0:T(2,128)(2,1)S(1)} %maximum_bitcast_fusion.1), channel_id=1, replica_groups=mesh['ctx'=64,'fsdp'=8] {'ctx'}, dimensions={0}, use_global_device_ids=true | all-gather | bytes 149760 | tf_op jit(solution)/shard_map/all_gather | solution.py:50
  240.3 3.5 collective-permute-done.8
  251.5 12.6 %collective-permute-start.6 = (bf16[192,512]{0,1:T(8,128)(2,1)S(1)}, bf16[192,512]{0,1:T(8,128)(2,1)}, u32[]{:S(2)}, u32[]{:S(2)}) collective-permute-start(bf16[192,512]{0,1:T(8,128)(2,1)S(1)} %copy.121), channel_id=1, source_target_pairs={{456,0},{464,8},{472,16},{480,24},{488,32},{496,40},{504,48},{0,56... | collective-permute-start | bytes 589832 | tf_op jit(solution)/shard_map/ppermute | solution.py:57
  264.1 6.4 %collective-permute-start.14 = (bf16[192,512]{1,0:T(8,128)(2,1)}, bf16[192,512]{1,0:T(8,128)(2,1)}, u32[]{:S(2)}, u32[]{:S(2)}) collective-permute-start(bf16[192,512]{1,0:T(8,128)(2,1)} %param.13), channel_id=1, source_target_pairs={{8,0},{16,8},{24,16},{32,24},{40,32},{48,40},{56,48},{64,56},{72,6... | collective-permute-start | bytes 589832 | tf_op jit(solution)/shard_map/ppermute | solution.py:57
  276.8 59.5 %psum.7 = f32[192,64]{0,1:T(8,128)} all-reduce(f32[192,64]{0,1:T(8,128)S(1)} %convolution_bitcast_fusion.5), channel_id=1, replica_groups=mesh['ctx'=64,'fsdp'=8] {'fsdp'}, use_global_device_ids=true, to_apply=%region_1.2 | all-reduce | flops 12288 | bytes 98304 | tf_op jit(solution)/shard_map/psum | solution.py:119
  344.8 2.7 concatenate.24
  347.5 3.0 collective-permute-start.19
  352.1 5.9 %collective-permute-start.20 = (bf16[192,512]{1,0:T(8,128)(2,1)}, bf16[192,512]{1,0:T(8,128)(2,1)}, u32[]{:S(2)}, u32[]{:S(2)}) collective-permute-start(bf16[192,512]{1,0:T(8,128)(2,1)} %param.13), channel_id=1, source_target_pairs={{56,0},{64,8},{72,16},{80,24},{88,32},{96,40},{104,48},{112,56},{1... | collective-permute-start | bytes 589832 | tf_op jit(solution)/shard_map/ppermute | solution.py:57
  366.5 3.2 copy.151
  369.7 4.3 convolution_bitcast_fusion.4
  377.4 38.9 %while.36 = (s32[]{:T(128)}, bf16[4,192,128]{2,1,0:T(8,128)(2,1)}, bf16[4,192,128]{2,1,0:T(8,128)(2,1)}, f32[4,192,128]{2,1,0:T(8,128)}, f32[4,192,128]{2,1,0:T(...) while((s32[]{:T(128)}, bf16[4,192,128]{2,1,0:T(8,128)(2,1)}, ...), condition=%wide.region_6.7_spmd.clone.clone, body=%wide.region_2.6_spmd.clone.clone.sunk | while | flops 327671424 | bytes 13357555 | solution.py:190
  423.3 4.3 collective-permute-start.36
  427.6 9.9 %collective-permute-start.37 = (f32[4,192]{1,0:T(4,128)S(1)}, f32[4,192]{1,0:T(4,128)S(1)}, u32[]{:S(2)}, u32[]{:S(2)}) collective-permute-start(f32[4,192]{1,0:T(4,128)S(1)} %copy-done.27), channel_id=1, source_target_pairs={{24,0},{32,8},{40,16},{48,24},{56,32},{64,40},{72,48},{80,56},{88,... | collective-permute-start | bytes 9224 | tf_op jit(solution)/shard_map/ppermute | solution.py:57
  437.5 3.1 collective-permute-start.38
  444.7 4.9 collective-permute-start.41
  449.7 4.3 collective-permute-start.21
  454.0 3.4 collective-permute-start.22
  459.6 3.7 collective-permute-start.24
  465.2 12.2 %all-to-all-start.1 = ((f32[8,192,64]{1,2,0:T(8,128)}), f32[8,192,64]{1,2,0:T(8,128)S(1)}, u32[]{:S(2)}, u32[]{:S(2)}) async-start(f32[8,192,64]{1,2,0:T(8,128)} %broadcast_in_dim.154), calls=%async_computation.1 | async-start | bytes 1048576 | tf_op jit(solution)/shard_map/all_to_all | solution.py:40
  483.8 3.8 collective-permute-start.28
  487.6 3.0 collective-permute-start.29
  494.3 7.7 %collective-permute-start.31 = (bf16[192,512]{1,0:T(8,128)(2,1)S(1)}, bf16[192,512]{1,0:T(8,128)(2,1)S(1)}, u32[]{:S(2)}, u32[]{:S(2)}) collective-permute-start(bf16[192,512]{1,0:T(8,128)(2,1)S(1)} %copy-done.11), channel_id=1, source_target_pairs={{32,0},{40,8},{48,16},{56,24},{64,32},{72,40},{80,48},{88,56},{96,... | collective-permute-start | bytes 589832 | tf_op jit(solution)/shard_map/ppermute | solution.py:57
  502.1 6.4 %collective-permute-start.32 = (bf16[192,512]{1,0:T(8,128)(2,1)S(1)}, bf16[192,512]{1,0:T(8,128)(2,1)S(1)}, u32[]{:S(2)}, u32[]{:S(2)}) collective-permute-start(bf16[192,512]{1,0:T(8,128)(2,1)S(1)} %copy-done.11), channel_id=1, source_target_pairs={{40,0},{48,8},{56,16},{64,24},{72,32},{80,40},{88,48},{96,56},{104... | collective-permute-start | bytes 589832 | tf_op jit(solution)/shard_map/ppermute | solution.py:57
  509.2 4.0 collective-permute-start.33
  517.6 4.5 collective-permute-done.34
  524.2 10.4 %all-to-all-start.2 = ((f32[64,1,1152]{2,1,0:T(1,128)}), f32[64,1,1152]{2,1,0:T(1,128)S(1)}, u32[]{:S(2)}, u32[]{:S(2)}) async-start(f32[64,1,1152]{2,1,0:T(1,128)} %copy.145), calls=%async_computation.2 | async-start | bytes 589824 | tf_op jit(solution)/shard_map/all_to_all | solution.py:72
  536.2 28.5 %while.37 = (s32[]{:T(128)}, f32[4,192,128]{2,1,0:T(8,128)}, f32[4,192,128]{2,1,0:T(8,128)}, pred[4]{0:T(512)(128)(4,1)}, bf16[4,1344,128]{2,1,0:T(8,128)(2,1)},...) while((s32[]{:T(128)}, f32[4,192,128]{2,1,0:T(8,128)}, ...), condition=%wide.region_8.9_spmd.clone.clone, body=%wide.region_7.8_spmd.clone.clone.sunk | while | flops 266353920 | bytes 4908036 | solution.py:234
  (272 shorter events, 160.4 us)
Async XLA Ops:
  7.2 362.6 %all-gather.3.cloned.1.call-start = ((), (), s32[]{:S(2)}) async-start(), calls=%async_computation.3 | async-start | bytes 5324800 | tf_op jit(solution)/shard_map/all_gather | solution.py:122
  12.6 353.9 %all-to-all-start = ((bf16[8,192,640]{2,1,0:T(8,128)(2,1)}), bf16[8,192,640]{2,1,0:T(8,128)(2,1)}, u32[]{:S(2)}, u32[]{:S(2)}) async-start(bf16[8,192,640]{2,1,0:T(8,128)(2,1)} %broadcast_in_dim.153), calls=%async_computation | async-start | bytes 3932160 | tf_op jit(solution)/shard_map/all_to_all | solution.py:40
  24.7 204.8 %collective-permute-start.10 = (bf16[192,512]{0,1:T(8,128)(2,1)S(1)}, bf16[192,512]{0,1:T(8,128)(2,1)S(1)}, u32[]{:S(2)}, u32[]{:S(2)}) collective-permute-start(bf16[192,512]{0,1:T(8,128)(2,1)S(1)} %copy.129), channel_id=1, source_target_pairs={{480,0},{488,8},{496,16},{504,24},{0,32},{8,40},{16,48},{24,56},{3... | collective-permute-start | bytes 589832 | tf_op jit(solution)/shard_map/ppermute | solution.py:57
  29.4 202.5 %collective-permute-start.11 = (bf16[192,512]{0,1:T(8,128)(2,1)S(1)}, bf16[192,512]{0,1:T(8,128)(2,1)S(1)}, u32[]{:S(2)}, u32[]{:S(2)}) collective-permute-start(bf16[192,512]{0,1:T(8,128)(2,1)S(1)} %copy.129), channel_id=1, source_target_pairs={{472,0},{480,8},{488,16},{496,24},{504,32},{0,40},{8,48},{16,56},{... | collective-permute-start | bytes 589832 | tf_op jit(solution)/shard_map/ppermute | solution.py:57
  33.4 200.4 %collective-permute-start.12 = (bf16[192,512]{0,1:T(8,128)(2,1)S(1)}, bf16[192,512]{0,1:T(8,128)(2,1)S(1)}, u32[]{:S(2)}, u32[]{:S(2)}) collective-permute-start(bf16[192,512]{0,1:T(8,128)(2,1)S(1)} %copy.129), channel_id=1, source_target_pairs={{464,0},{472,8},{480,16},{488,24},{496,32},{504,40},{0,48},{8,56},... | collective-permute-start | bytes 589832 | tf_op jit(solution)/shard_map/ppermute | solution.py:57
  37.8 197.9 %collective-permute-start.13 = (bf16[192,512]{0,1:T(8,128)(2,1)S(1)}, bf16[192,512]{0,1:T(8,128)(2,1)S(1)}, u32[]{:S(2)}, u32[]{:S(2)}) collective-permute-start(bf16[192,512]{0,1:T(8,128)(2,1)S(1)} %copy.129), channel_id=1, source_target_pairs={{456,0},{464,8},{472,16},{480,24},{488,32},{496,40},{504,48},{0,56... | collective-permute-start | bytes 589832 | tf_op jit(solution)/shard_map/ppermute | solution.py:57
  40.4 197.3 %collective-permute-start.7 = (bf16[192,512]{0,1:T(8,128)(2,1)S(1)}, bf16[192,512]{0,1:T(8,128)(2,1)S(1)}, u32[]{:S(2)}, u32[]{:S(2)}) collective-permute-start(bf16[192,512]{0,1:T(8,128)(2,1)S(1)} %copy.129), channel_id=1, source_target_pairs={{504,0},{0,8},{8,16},{16,24},{24,32},{32,40},{40,48},{48,56},{56,6... | collective-permute-start | bytes 589832 | tf_op jit(solution)/shard_map/ppermute | solution.py:57
  237.7 26.4 %collective-permute-start.2 = (bf16[192,512]{0,1:T(8,128)(2,1)S(1)}, bf16[192,512]{0,1:T(8,128)(2,1)S(1)}, u32[]{:S(2)}, u32[]{:S(2)}) collective-permute-start(bf16[192,512]{0,1:T(8,128)(2,1)S(1)} %copy.121), channel_id=1, source_target_pairs={{488,0},{496,8},{504,16},{0,24},{8,32},{16,40},{24,48},{32,56},{40... | collective-permute-start | bytes 589832 | tf_op jit(solution)/shard_map/ppermute | solution.py:57
  243.8 27.3 %collective-permute-start.3 = (bf16[192,512]{0,1:T(8,128)(2,1)S(1)}, bf16[192,512]{0,1:T(8,128)(2,1)S(1)}, u32[]{:S(2)}, u32[]{:S(2)}) collective-permute-start(bf16[192,512]{0,1:T(8,128)(2,1)S(1)} %copy.121), channel_id=1, source_target_pairs={{480,0},{488,8},{496,16},{504,24},{0,32},{8,40},{16,48},{24,56},{3... | collective-permute-start | bytes 589832 | tf_op jit(solution)/shard_map/ppermute | solution.py:57
  246.4 92.6 %collective-permute-start.4 = (bf16[192,512]{0,1:T(8,128)(2,1)S(1)}, bf16[192,512]{0,1:T(8,128)(2,1)}, u32[]{:S(2)}, u32[]{:S(2)}) collective-permute-start(bf16[192,512]{0,1:T(8,128)(2,1)S(1)} %copy.121), channel_id=1, source_target_pairs={{472,0},{480,8},{488,16},{496,24},{504,32},{0,40},{8,48},{16,56},{... | collective-permute-start | bytes 589832 | tf_op jit(solution)/shard_map/ppermute | solution.py:57
  249.5 91.3 %collective-permute-start.5 = (bf16[192,512]{0,1:T(8,128)(2,1)S(1)}, bf16[192,512]{0,1:T(8,128)(2,1)}, u32[]{:S(2)}, u32[]{:S(2)}) collective-permute-start(bf16[192,512]{0,1:T(8,128)(2,1)S(1)} %copy.121), channel_id=1, source_target_pairs={{464,0},{472,8},{480,16},{488,24},{496,32},{504,40},{0,48},{8,56},... | collective-permute-start | bytes 589832 | tf_op jit(solution)/shard_map/ppermute | solution.py:57
  251.5 91.3 %collective-permute-start.6 = (bf16[192,512]{0,1:T(8,128)(2,1)S(1)}, bf16[192,512]{0,1:T(8,128)(2,1)}, u32[]{:S(2)}, u32[]{:S(2)}) collective-permute-start(bf16[192,512]{0,1:T(8,128)(2,1)S(1)} %copy.121), channel_id=1, source_target_pairs={{456,0},{464,8},{472,16},{480,24},{488,32},{496,40},{504,48},{0,56... | collective-permute-start | bytes 589832 | tf_op jit(solution)/shard_map/ppermute | solution.py:57
  264.1 83.3 %collective-permute-start.14 = (bf16[192,512]{1,0:T(8,128)(2,1)}, bf16[192,512]{1,0:T(8,128)(2,1)}, u32[]{:S(2)}, u32[]{:S(2)}) collective-permute-start(bf16[192,512]{1,0:T(8,128)(2,1)} %param.13), channel_id=1, source_target_pairs={{8,0},{16,8},{24,16},{32,24},{40,32},{48,40},{56,48},{64,56},{72,6... | collective-permute-start | bytes 589832 | tf_op jit(solution)/shard_map/ppermute | solution.py:57
  271.1 81.0 %collective-permute-start.15 = (bf16[192,512]{1,0:T(8,128)(2,1)}, bf16[192,512]{1,0:T(8,128)(2,1)}, u32[]{:S(2)}, u32[]{:S(2)}) collective-permute-start(bf16[192,512]{1,0:T(8,128)(2,1)} %param.13), channel_id=1, source_target_pairs={{16,0},{24,8},{32,16},{40,24},{48,32},{56,40},{64,48},{72,56},{80,... | collective-permute-start | bytes 589832 | tf_op jit(solution)/shard_map/ppermute | solution.py:57
  338.9 20.7 %collective-permute-start.16 = (bf16[192,512]{1,0:T(8,128)(2,1)}, bf16[192,512]{1,0:T(8,128)(2,1)}, u32[]{:S(2)}, u32[]{:S(2)}) collective-permute-start(bf16[192,512]{1,0:T(8,128)(2,1)} %param.13), channel_id=1, source_target_pairs={{24,0},{32,8},{40,16},{48,24},{56,32},{64,40},{72,48},{80,56},{88,... | collective-permute-start | bytes 589832 | tf_op jit(solution)/shard_map/ppermute | solution.py:57
  340.9 20.4 %collective-permute-start.17 = (bf16[192,512]{1,0:T(8,128)(2,1)}, bf16[192,512]{1,0:T(8,128)(2,1)}, u32[]{:S(2)}, u32[]{:S(2)}) collective-permute-start(bf16[192,512]{1,0:T(8,128)(2,1)} %param.13), channel_id=1, source_target_pairs={{32,0},{40,8},{48,16},{56,24},{64,32},{72,40},{80,48},{88,56},{96,... | collective-permute-start | bytes 589832 | tf_op jit(solution)/shard_map/ppermute | solution.py:57
  352.1 66.1 %collective-permute-start.20 = (bf16[192,512]{1,0:T(8,128)(2,1)}, bf16[192,512]{1,0:T(8,128)(2,1)}, u32[]{:S(2)}, u32[]{:S(2)}) collective-permute-start(bf16[192,512]{1,0:T(8,128)(2,1)} %param.13), channel_id=1, source_target_pairs={{56,0},{64,8},{72,16},{80,24},{88,32},{96,40},{104,48},{112,56},{1... | collective-permute-start | bytes 589832 | tf_op jit(solution)/shard_map/ppermute | solution.py:57
  416.3 26.3 %collective-permute-start.35 = (f32[4,192]{1,0:T(4,128)}, f32[4,192]{1,0:T(4,128)S(1)}, u32[]{:S(2)}, u32[]{:S(2)}) collective-permute-start(f32[4,192]{1,0:T(4,128)} %get-tuple-element.148), channel_id=1, source_target_pairs={{8,0},{16,8},{24,16},{32,24},{40,32},{48,40},{56,48},{64,56},{72,6... | collective-permute-start | bytes 9224 | tf_op jit(solution)/shard_map/ppermute | solution.py:57
  423.3 21.4 %collective-permute-start.36 = (f32[4,192]{1,0:T(4,128)S(1)}, f32[4,192]{1,0:T(4,128)S(1)}, u32[]{:S(2)}, u32[]{:S(2)}) collective-permute-start(f32[4,192]{1,0:T(4,128)S(1)} %copy-done.27), channel_id=1, source_target_pairs={{16,0},{24,8},{32,16},{40,24},{48,32},{56,40},{64,48},{72,56},{80,... | collective-permute-start | bytes 9224 | tf_op jit(solution)/shard_map/ppermute | solution.py:57
  427.6 22.0 %collective-permute-start.37 = (f32[4,192]{1,0:T(4,128)S(1)}, f32[4,192]{1,0:T(4,128)S(1)}, u32[]{:S(2)}, u32[]{:S(2)}) collective-permute-start(f32[4,192]{1,0:T(4,128)S(1)} %copy-done.27), channel_id=1, source_target_pairs={{24,0},{32,8},{40,16},{48,24},{56,32},{64,40},{72,48},{80,56},{88,... | collective-permute-start | bytes 9224 | tf_op jit(solution)/shard_map/ppermute | solution.py:57
  444.7 32.7 %collective-permute-start.41 = (f32[4,192]{1,0:T(4,128)S(1)}, f32[4,192]{1,0:T(4,128)S(1)}, u32[]{:S(2)}, u32[]{:S(2)}) collective-permute-start(f32[4,192]{1,0:T(4,128)S(1)} %copy-done.27), channel_id=1, source_target_pairs={{56,0},{64,8},{72,16},{80,24},{88,32},{96,40},{104,48},{112,56},{1... | collective-permute-start | bytes 9224 | tf_op jit(solution)/shard_map/ppermute | solution.py:57
  449.7 29.7 %collective-permute-start.21 = (f32[4,192]{1,0:T(4,128)S(1)}, f32[4,192]{1,0:T(4,128)S(1)}, u32[]{:S(2)}, u32[]{:S(2)}) collective-permute-start(f32[4,192]{1,0:T(4,128)S(1)} %copy-done.26), channel_id=1, source_target_pairs={{8,0},{16,8},{24,16},{32,24},{40,32},{48,40},{56,48},{64,56},{72,6... | collective-permute-start | bytes 9224 | tf_op jit(solution)/shard_map/ppermute | solution.py:57
  454.0 27.3 %collective-permute-start.22 = (f32[4,192]{1,0:T(4,128)S(1)}, f32[4,192]{1,0:T(4,128)S(1)}, u32[]{:S(2)}, u32[]{:S(2)}) collective-permute-start(f32[4,192]{1,0:T(4,128)S(1)} %copy-done.26), channel_id=1, source_target_pairs={{16,0},{24,8},{32,16},{40,24},{48,32},{56,40},{64,48},{72,56},{80,... | collective-permute-start | bytes 9224 | tf_op jit(solution)/shard_map/ppermute | solution.py:57
  457.4 26.4 %collective-permute-start.23 = (f32[4,192]{1,0:T(4,128)S(1)}, f32[4,192]{1,0:T(4,128)S(1)}, u32[]{:S(2)}, u32[]{:S(2)}) collective-permute-start(f32[4,192]{1,0:T(4,128)S(1)} %copy-done.26), channel_id=1, source_target_pairs={{24,0},{32,8},{40,16},{48,24},{56,32},{64,40},{72,48},{80,56},{88,... | collective-permute-start | bytes 9224 | tf_op jit(solution)/shard_map/ppermute | solution.py:57
  459.6 27.9 %collective-permute-start.24 = (f32[4,192]{1,0:T(4,128)S(1)}, f32[4,192]{1,0:T(4,128)S(1)}, u32[]{:S(2)}, u32[]{:S(2)}) collective-permute-start(f32[4,192]{1,0:T(4,128)S(1)} %copy-done.26), channel_id=1, source_target_pairs={{32,0},{40,8},{48,16},{56,24},{64,32},{72,40},{80,48},{88,56},{96,... | collective-permute-start | bytes 9224 | tf_op jit(solution)/shard_map/ppermute | solution.py:57
  465.2 57.1 %all-to-all-start.1 = ((f32[8,192,64]{1,2,0:T(8,128)}), f32[8,192,64]{1,2,0:T(8,128)S(1)}, u32[]{:S(2)}, u32[]{:S(2)}) async-start(f32[8,192,64]{1,2,0:T(8,128)} %broadcast_in_dim.154), calls=%async_computation.1 | async-start | bytes 1048576 | tf_op jit(solution)/shard_map/all_to_all | solution.py:40
  481.3 20.8 %collective-permute-start.27 = (f32[4,192]{1,0:T(4,128)S(1)}, f32[4,192]{1,0:T(4,128)S(1)}, u32[]{:S(2)}, u32[]{:S(2)}) collective-permute-start(f32[4,192]{1,0:T(4,128)S(1)} %copy-done.26), channel_id=1, source_target_pairs={{56,0},{64,8},{72,16},{80,24},{88,32},{96,40},{104,48},{112,56},{1... | collective-permute-start | bytes 9224 | tf_op jit(solution)/shard_map/ppermute | solution.py:57
  483.8 25.4 %collective-permute-start.28 = (bf16[192,512]{1,0:T(8,128)(2,1)S(1)}, bf16[192,512]{1,0:T(8,128)(2,1)S(1)}, u32[]{:S(2)}, u32[]{:S(2)}) collective-permute-start(bf16[192,512]{1,0:T(8,128)(2,1)S(1)} %copy-done.11), channel_id=1, source_target_pairs={{8,0},{16,8},{24,16},{32,24},{40,32},{48,40},{56,48},{64,56},{72,6... | collective-permute-start | bytes 589832 | tf_op jit(solution)/shard_map/ppermute | solution.py:57
  487.6 25.6 %collective-permute-start.29 = (bf16[192,512]{1,0:T(8,128)(2,1)S(1)}, bf16[192,512]{1,0:T(8,128)(2,1)S(1)}, u32[]{:S(2)}, u32[]{:S(2)}) collective-permute-start(bf16[192,512]{1,0:T(8,128)(2,1)S(1)} %copy-done.11), channel_id=1, source_target_pairs={{16,0},{24,8},{32,16},{40,24},{48,32},{56,40},{64,48},{72,56},{80,... | collective-permute-start | bytes 589832 | tf_op jit(solution)/shard_map/ppermute | solution.py:57
  492.0 23.5 %collective-permute-start.30 = (bf16[192,512]{1,0:T(8,128)(2,1)S(1)}, bf16[192,512]{1,0:T(8,128)(2,1)S(1)}, u32[]{:S(2)}, u32[]{:S(2)}) collective-permute-start(bf16[192,512]{1,0:T(8,128)(2,1)S(1)} %copy-done.11), channel_id=1, source_target_pairs={{24,0},{32,8},{40,16},{48,24},{56,32},{64,40},{72,48},{80,56},{88,... | collective-permute-start | bytes 589832 | tf_op jit(solution)/shard_map/ppermute | solution.py:57
  494.3 21.2 %collective-permute-start.31 = (bf16[192,512]{1,0:T(8,128)(2,1)S(1)}, bf16[192,512]{1,0:T(8,128)(2,1)S(1)}, u32[]{:S(2)}, u32[]{:S(2)}) collective-permute-start(bf16[192,512]{1,0:T(8,128)(2,1)S(1)} %copy-done.11), channel_id=1, source_target_pairs={{32,0},{40,8},{48,16},{56,24},{64,32},{72,40},{80,48},{88,56},{96,... | collective-permute-start | bytes 589832 | tf_op jit(solution)/shard_map/ppermute | solution.py:57
  524.2 43.9 %all-to-all-start.2 = ((f32[64,1,1152]{2,1,0:T(1,128)}), f32[64,1,1152]{2,1,0:T(1,128)S(1)}, u32[]{:S(2)}, u32[]{:S(2)}) async-start(f32[64,1,1152]{2,1,0:T(1,128)} %copy.145), calls=%async_computation.2 | async-start | bytes 589824 | tf_op jit(solution)/shard_map/all_to_all | solution.py:72
  (48 other events, 1034.1 us)
Sparse Core Ops, SparseCore 0:
  11.2 319.1 all-gather.2
where the time goes:
time: 580 us; the launch traced here: 576 us
  blocking collectives  245 us (42%)
  starting transfers between devices  182 us (31%)
  local copies, waits for them, and re-layouts  61.5 us (11%)
  matrix products  45.2 us (8%)
  between operations  15 us (3%)
  other arithmetic  14.6 us (3%)
  waiting for transfers between devices  12.6 us (2%)
    all_gather x1, blocking collectives, side_by_side(): result = lax.all_gather(both, axis, axis=dim, tiled=True)  185 us
    ppermute x42, starting transfers between devices, passed_along(): return lax.ppermute(block, axis, route)  148 us
    psum x1, blocking collectives, on_device(): lax.psum(backward_piece, 'fsdp')  59.5 us
    all_to_all x2, starting transfers between devices, copy_for_each(): return lax.all_to_all(copies, axis, split_axis=0, concat_axis=0, tiled=True)  24.1 us
    unnamed x72, local copies, waits for them, and re-layouts  15.1 us
    ppermute x42, waiting for transfers between devices, passed_along(): return lax.ppermute(block, axis, route)  12.6 us
  transfers between devices with their start and end apart: 46, of which 5 were waited for; matrix products, arithmetic and copies ran while one was open for 20% of the time, Pallas kernels for 0%

commit v1 on v0

v1 whole, which is shorter than its diff:
```python
import jax
import jax.numpy as jnp
from jax import lax
from jax.experimental import pallas as pl
from jax.experimental.pallas import tpu as pltpu
from jax.sharding import PartitionSpec as P

HEAD_WIDTH = 128
MESH = pl.DeviceIdType.MESH
BLOCK = 384
nf4_values = (
    -1.0,
    -0.6961928009986877,
    -0.5250730514526367,
    -0.39491748809814453,
    -0.28444138169288635,
    -0.18477343022823334,
    -0.09105003625154495,
    0.0,
    0.07958029955625534,
    0.16093020141124725,
    0.24611230194568634,
    0.33791524171829224,
    0.44070982933044434,
    0.5626170039176941,
    0.7229568362236023,
    1.0,
)
adapter_scale = 0.25
masked = -1e30
f32, bf16 = jnp.float32, jnp.bfloat16
SEMS = 256


def dequantize(frozen_weight_codes, block_scale_index, block_scale_table):
    values = jnp.zeros(frozen_weight_codes.shape, f32)
    for level_code in range(16):
        values = values + jnp.where(frozen_weight_codes == level_code, nf4_values[level_code], 0.0)
    level_iota = lax.broadcasted_iota(jnp.int32, (1, 1, block_scale_table.shape[0]), 2)
    picked = jnp.sum(
        jnp.where(block_scale_index[:, :, None] == level_iota, block_scale_table, 0.0), axis=-1
    )
    scales = jnp.repeat(picked, frozen_weight_codes.shape[1] // block_scale_index.shape[1], axis=1)
    return (values * scales).astype(bf16)


def nt(a, b):
    return lax.dot_general(a, b, (((1,), (1,)), ((), ())), preferred_element_type=f32)


def tn(a, b):
    return lax.dot_general(a, b, (((0,), (0,)), ((), ())), preferred_element_type=f32)


def nn(a, b):
    return jnp.dot(a, b, preferred_element_type=f32)


def kernel(
    q_ref, k_ref, v_ref, g_ref, w_ref, ad_ref, au_ref,
    dq_ref, dk_ref, dv_ref, dn_ref, up_ref,
    WA, WB, GB, QU, KU, VU, DU, PT, KT, OB, OS, DQS, DKS, DVS, DKA, DVA, DOB,
    AD1, AD2, PSS, PSR, PSG, UPD, R1, S2, R2, ss, rs, ls,
):
    ctx = lax.axis_index("ctx")
    f = lax.axis_index("fsdp")
    y, g = ctx // 8, ctx % 8
    x, zl = g // 2, g % 2
    c = f % 2
    partner = f + 1 - 2 * c
    scale = HEAD_WIDTH ** (-0.5)
    is_host = (x % 2) == c
    unit_head = 2 * (x // 2) + zl

    counter = [0]
    sends = []

    def ids(n):
        first = counter[0]
        counter[0] += n
        return first

    def remote(src, dst, sem, to_ctx, to_f, recv=None):
        return pltpu.make_async_remote_copy(
            src_ref=src,
            dst_ref=dst,
            send_sem=ss.at[sem],
            recv_sem=rs.at[sem if recv is None else recv],
            device_id={"ctx": to_ctx, "fsdp": to_f},
            device_id_type=MESH,
        )

    def go(src, dst, sem, to_ctx, to_f):
        copy = remote(src, dst, sem, to_ctx, to_f)
        copy.start()
        sends.append(copy)
        return copy

    def arrived(dst, sem):
        pltpu.make_async_copy(dst, dst, rs.at[sem]).wait()

    def row(dy):
        return (y + dy) % 8

    def at(yy, gg):
        return yy * 8 + gg

    def ydev(dy):
        return at(row(dy), g)

    def xdev(dx):
        return at(y, ((x + dx) % 4) * 2 + zl)

    def fdev(df):
        return (f + df) % 8

    other_row = jnp.where(x < 2, (y + 7) % 8, (y + 1) % 8)
    other_g = jnp.where(x < 2, 4, 0)

    barrier = pltpu.get_barrier_semaphore()
    peers = [(at(y, (g + j) % 8), f) for j in range(1, 8)]
    peers += [(ydev(j), f) for j in range(1, 8)]
    peers += [(ctx, fdev(j)) for j in range(1, 8)]
    peers += [(at(other_row, other_g + j), f) for j in range(4)]
    for to_ctx, to_f in peers:
        pl.semaphore_signal(
            barrier, inc=1, device_id={"ctx": to_ctx, "fsdp": to_f}, device_id_type=MESH
        )
    pl.semaphore_wait(barrier, len(peers))

    pair = ctx + 1 - 2 * zl
    i = ids(2)
    wl, wr = w_ref.at[:, 0:256], w_ref.at[:, 256:512]
    s1 = [go(wl, WA.at[y, g], i, pair, f), go(wr, WB.at[y, g], i + 1, pair, f)]
    own_copies = [
        pltpu.make_async_copy(wl, WA.at[y, g], ls.at[0]),
        pltpu.make_async_copy(wr, WB.at[y, g], ls.at[1]),
        pltpu.make_async_copy(g_ref, GB.at[f], ls.at[2]),
    ]
    for copy in own_copies:
        copy.start()

    gi = ids(11)
    half = [pl.ds(0, 96), pl.ds(96, 96)]
    go(g_ref, GB.at[f], gi, ctx, partner)
    go(g_ref, GB.at[f], gi + 1, ctx, fdev(2))
    go(g_ref, GB.at[f], gi + 2, ctx, fdev(6))

    AD1[g] = jnp.concatenate([ad_ref[...].astype(f32), au_ref[...].astype(f32)], axis=1)
    ai = ids(8)
    for j in range(1, 8):
        go(AD1.at[g], AD1.at[g], ai + j, at(y, (g + j) % 8), f)

    def slab_of(head):
        if head < 2:
            return y, g
        return jnp.where(x < 2, (y + 7) % 8, y), (g + 4) % 8

    def host_of(head):
        yy, _ = slab_of(head)
        return at(yy, (2 * (head // 2) + c) * 2 + head % 2)

    conditional = []

    def to_hosts(src_ref, dst_buf, recv_base):
        send_base = ids(4)
        for head in range(4):
            dest = host_of(head)
            _, slot = slab_of(head)
            src = src_ref.at[:, head * 128 : (head + 1) * 128]
            dst = dst_buf.at[slot]
            away = dest != ctx
            copy = remote(src, dst, send_base + head, dest, f, recv_base + slot)

            @pl.when(away)
            def _():
                copy.start()

            @pl.when(jnp.logical_not(away))
            def _():
                pltpu.make_async_copy(src, dst, rs.at[recv_base + slot]).start()

            conditional.append((away, copy))

    ki, qi, vi, di = ids(8), ids(8), ids(8), ids(8)
    to_hosts(k_ref, KU, ki)
    to_hosts(q_ref, QU, qi)
    to_hosts(v_ref, VU, vi)

    for copy in own_copies:
        copy.wait()
    for copy in s1:
        copy.wait_recv()

    def PB(dy, dx):
        return WB.at[row(dy), pl.ds(((x + dx) % 4) * 2, 2)]

    def QA(dy, h):
        return WA.at[row(dy), pl.ds(4 * h, 4)]

    yb = {d: ids(1) for d in (-4, -3, -2, -1, 1, 2, 3)}
    xb = {(s, d): ids(1) for s in (-1, 1) for d in range(-4, 4)}
    xr = {d: ids(1) for d in range(-4, 4)}
    up_relay = (-2, -1, 0, 1)

    def b_to_x(d):
        go(PB(d, 0), PB(d, 0), xb[(-1, d)], xdev(1), f)
        go(PB(d, 0), PB(d, 0), xb[(1, d)], xdev(-1), f)

    def b_up(d):
        go(PB(d, 0), PB(d, 0), yb[d - 1], ydev(1), f)

    def b_down(d):
        go(PB(d, 0), PB(d, 0), yb[d + 1], ydev(-1), f)

    def b_arrived(d):
        arrived(PB(d, 0), yb[d])

    def x_relay(d):
        side = -1 if d in up_relay else 1
        arrived(PB(d, side), xb[(side, d)])
        go(PB(d, side), PB(d, side), xr[d], xdev(-side), f)

    b_up(0)
    b_down(0)
    mine = WA.at[y, pl.ds(x * 2, 2)]
    xa = ids(3)
    go(mine, mine, xa, xdev(1), f)
    go(mine, mine, xa + 1, xdev(-1), f)
    go(mine, mine, xa + 2, xdev(2), f)
    b_to_x(0)

    for j in range(1, 8):
        arrived(AD1.at[(g + 8 - j) % 8], ai + j)
    AD2[y] = jnp.concatenate([AD1[j] for j in range(8)], axis=0)
    bi = ids(8)
    for j in range(1, 8):
        go(AD2.at[y], AD2.at[y], bi + j, ydev(j), f)

    for k, dx in enumerate((-1, 1, 2)):
        block = WA.at[y, pl.ds(((x + dx) % 4) * 2, 2)]
        arrived(block, xa + k)

    ya = {(d, h): ids(1) for d in (-4, -3, -2, -1, 1, 2, 3, 4) for h in (0, 1)}

    def a_up(d, h):
        go(QA(d, h), QA(d, h), ya[(d - 1, h)], ydev(1), f)

    def a_down(d, h):
        go(QA(d, h), QA(d, h), ya[(d + 1, h)], ydev(-1), f)

    def a_arrived(d, h):
        arrived(QA(d, h), ya[(d, h)])

    for h in (0, 1):
        a_up(0, h)
        a_down(0, h)

    def b_step(d):
        b_arrived(-d)
        b_up(-d)
        b_to_x(-d)
        b_arrived(d)
        if d < 3:
            b_down(d)
        b_to_x(d)

    b_step(1)
    x_relay(0)

    below, above, across = fdev(6), fdev(2), fdev(4)
    arrived(GB.at[below], gi + 1)
    go(GB.at[below, half[0]], GB.at[below, half[0]], gi + 3, ctx, above)
    go(GB.at[below], GB.at[below], gi + 4, ctx, partner)
    arrived(GB.at[above], gi + 2)
    go(GB.at[above, half[1]], GB.at[above, half[1]], gi + 5, ctx, below)
    go(GB.at[above], GB.at[above], gi + 6, ctx, partner)

    b_step(2)
    x_relay(-1)
    x_relay(1)
    for h in (0, 1):
        a_arrived(-1, h)
        a_up(-1, h)
        a_arrived(1, h)
        a_down(1, h)

    def sum_start(n, piece):
        PSS[n] = piece.reshape(8, 24, 128)
        base = ids(8)
        for j in range(1, 8):
            to = fdev(j)
            go(PSS.at[n, to], PSR.at[n, f], base + j, ctx, to)
        return base

    def sum_middle(n, base, factor):
        total = PSS[n, f]
        for j in range(1, 8):
            frm = fdev(8 - j)
            arrived(PSR.at[n, frm], base + j)
            total = total + PSR[n, frm]
        PSG[n, f] = (total * factor).astype(bf16).astype(f32)
        base = ids(8)
        for j in range(1, 8):
            go(PSG.at[n, f], PSG.at[n, f], base + j, ctx, fdev(j))
        return base

    def sum_end(n, base):
        for j in range(1, 8):
            arrived(PSG.at[n, fdev(8 - j)], base + j)
        return PSG[n].reshape(192, 128).astype(bf16)

    for j in range(1, 8):
        arrived(AD2.at[row(8 - j)], bi + j)
    adapters = AD2[...].reshape(64, 1152).astype(bf16)
    adapters = jnp.concatenate([adapters, jnp.zeros_like(adapters)], axis=0)
    down_full, up_piece = adapters[:, :512], adapters[:, 512:]
    back_base = sum_start(0, nt(g_ref[...], up_piece))

    b_step(3)
    x_relay(-2)
    x_relay(2)

    oi = ids(4)
    oh = ids(8)

    def source_of(slot):
        if slot < 4:
            return jnp.where(x < 2, at(y, slot), at(y, slot + 4))
        return jnp.where(x < 2, at(y, slot), at(row(1), slot - 4))

    head_columns = pl.ds(pl.multiple_of(unit_head * 128, 128), 128)
    hosted = []

    def returned(buf, dst_ref, recv_base, send_sem, slot):
        dest = source_of(slot)
        src, dst = buf.at[slot], dst_ref.at[:, head_columns]
        copy = remote(src, dst, send_sem, dest, f, recv_base + unit_head)
        return dest != ctx, copy, src, dst

    def from_host(*what):
        away, copy, src, dst = returned(*what)
        recv_base = what[2]

        @pl.when(away)
        def _():
            copy.start()

        @pl.when(jnp.logical_not(away))
        def _():
            pltpu.make_async_copy(src, dst, rs.at[recv_base + unit_head]).start()

        hosted.append(what)

    blocks = 8 // (BLOCK // 192)

    def two(buf, b):
        return buf[2 * b : 2 * b + 2].reshape(BLOCK, 128)

    def tile(b, kb):
        return b * (b + 1) // 2 + kb

    @pl.when(is_host)
    def _():
        for s in range(8):
            arrived(KU.at[s], ki + s)
            arrived(QU.at[s], qi + s)
        key_at = lax.broadcasted_iota(jnp.int32, (BLOCK, BLOCK), 0)
        query_at = lax.broadcasted_iota(jnp.int32, (BLOCK, BLOCK), 1)
        seen = key_at <= query_at
        for s in range(8):
            arrived(VU.at[s], vi + s)
        for b in range(blocks):
            query = two(QU, b)
            parts = []
            for kb in range(b + 1):
                part = nt(two(KU, kb), query) * scale
                parts.append(jnp.where(seen, part, masked) if kb == b else part)
            top = jnp.max(parts[0], axis=0, keepdims=True)
            for part in parts[1:]:
                top = jnp.maximum(top, jnp.max(part, axis=0, keepdims=True))
            parts = [jnp.exp(part - top) for part in parts]
            total = jnp.sum(parts[0], axis=0, keepdims=True)
            for part in parts[1:]:
                total = total + jnp.sum(part, axis=0, keepdims=True)
            inverse = 1.0 / total
            out = jnp.zeros((BLOCK, 128), f32)
            for kb in range(b + 1):
                prob = parts[kb] * inverse
                PT[tile(b, kb)] = prob
                out = out + tn(prob.astype(bf16), two(VU, kb))
            OS[2 * b : 2 * b + 2] = out.astype(bf16).reshape(2, 192, 128)
            for s in (2 * b, 2 * b + 1):
                from_host(OS, OB, oi, oh + s, s)

    b_arrived(-4)
    b_to_x(-4)
    for h in (0, 1):
        a_arrived(-2, h)
        a_up(-2, h)
        a_arrived(2, h)
        a_down(2, h)
    x_relay(-3)
    x_relay(3)
    x_relay(-4)

    arrived(GB.at[across, half[0]], gi + 3)
    go(GB.at[across, half[0]], GB.at[across, half[0]], gi + 7, ctx, partner)
    arrived(GB.at[across, half[1]], gi + 5)
    go(GB.at[across, half[1]], GB.at[across, half[1]], gi + 8, ctx, partner)
    back_base = sum_middle(0, back_base, adapter_scale)

    a_arrived(-3, 0)
    a_up(-3, 0)
    a_arrived(-3, 1)
    a_arrived(3, 1)
    a_down(3, 1)
    a_arrived(3, 0)

    for head in range(4):
        arrived(OB.at[:, head * 128 : (head + 1) * 128], oi + head)
    mid_base = sum_start(1, nt(OB[...], down_full))
    lora_back = sum_end(0, back_base)

    arrived(GB.at[partner], gi)
    arrived(GB.at[(partner + 6) % 8], gi + 4)
    arrived(GB.at[(partner + 2) % 8], gi + 6)
    arrived(GB.at[(partner + 4) % 8, half[0]], gi + 7)
    arrived(GB.at[(partner + 4) % 8, half[1]], gi + 8)

    def a_part(d):
        yy = row(d)
        return nn(GB[yy], WA[yy].reshape(640, 256))

    total_a = nn(lora_back, down_full[:, :256])
    total_b = nn(lora_back, down_full[:, 256:])
    for d in (0, -1, 1, -2, 2, -3, 3):
        total_a = total_a + a_part(d)

    mid_base = sum_middle(1, mid_base, 1.0)

    a_arrived(-4, 0)
    a_arrived(4, 1)
    total_a = total_a + a_part(4)
    DOB[:, 0:256] = total_a.astype(bf16)

    for d in range(-4, 4):
        far = 1 if d in up_relay else -1
        arrived(PB(d, far), xb[(far, d)])
        arrived(PB(d, 2), xr[d])
    for yy in range(8):
        total_b = total_b + nn(GB[yy], WB[yy].reshape(640, 256))
    DOB[:, 256:512] = total_b.astype(bf16)
    to_hosts(DOB, DU, di)

    lora_mid = sum_end(1, mid_base)
    UPD[:, :, 0:512] = tn(lora_back, OB[...])[:64].reshape(8, 8, 512)
    UPD[:, :, 512:1152] = (adapter_scale * tn(lora_mid, g_ref[...]))[:64].reshape(8, 8, 640)
    ri = ids(8)
    for j in range(1, 8):
        go(UPD.at[row(j)], R1.at[y], ri + j, ydev(j), f)

    gq, gk, gv = ids(4), ids(4), ids(4)
    hq, hk, hv = ids(8), ids(8), ids(8)

    @pl.when(is_host)
    def _():
        for kb in range(blocks):
            KT[:, kb * BLOCK : (kb + 1) * BLOCK] = two(KU, kb).astype(f32).T.astype(bf16)
        DKA[...] = jnp.zeros_like(DKA)
        DVA[...] = jnp.zeros_like(DVA)
        for s in range(8):
            arrived(DU.at[s], di + s)
        for b in reversed(range(blocks)):
            grad, query = two(DU, b), two(QU, b)
            parts = []
            delta = jnp.zeros((1, BLOCK), f32)
            for kb in range(b + 1):
                part = nt(two(VU, kb), grad)
                delta = delta + jnp.sum(PT[tile(b, kb)] * part, axis=0, keepdims=True)
                parts.append(part)
            turned = jnp.zeros((128, BLOCK), f32)
            for kb in range(b + 1):
                span = pl.ds(kb * BLOCK, BLOCK)
                prob = PT[tile(b, kb)]
                pull = (prob * (parts[kb] - delta) * scale).astype(bf16)
                DKA[span] += nn(pull, query)
                DVA[span] += nn(prob.astype(bf16), grad)
                turned = turned + nn(KT[:, span], pull)
            span = pl.ds(b * BLOCK, BLOCK)
            DQS[2 * b : 2 * b + 2] = turned.T.astype(bf16).reshape(2, 192, 128)
            DKS[2 * b : 2 * b + 2] = DKA[span].astype(bf16).reshape(2, 192, 128)
            DVS[2 * b : 2 * b + 2] = DVA[span].astype(bf16).reshape(2, 192, 128)
            for s in (2 * b, 2 * b + 1):
                from_host(DQS, dq_ref, gq, hq + s, s)
                from_host(DKS, dk_ref, gk, hk + s, s)
                from_host(DVS, dv_ref, gv, hv + s, s)

    total = UPD[y]
    for j in range(1, 8):
        frm = row(8 - j)
        arrived(R1.at[frm], ri + j)
        total = total + R1[frm]
    for j in range(8):
        S2[j] = total[j : j + 1]
    ti = ids(8)
    for j in range(1, 8):
        to = (g + j) % 8
        go(S2.at[to], R2.at[g], ti + j, at(y, to), f)
    total = S2[g]
    for j in range(1, 8):
        frm = (g + 8 - j) % 8
        arrived(R2.at[frm], ti + j)
        total = total + R2[frm]
    dn_ref[...] = total[:, 0:512]
    up_ref[...] = total[:, 512:1152]

    for head in range(4):
        span = slice(head * 128, (head + 1) * 128)
        arrived(dq_ref.at[:, span], gq + head)
        arrived(dk_ref.at[:, span], gk + head)
        arrived(dv_ref.at[:, span], gv + head)

    for copy in sends:
        copy.wait_send()
    for away, copy in conditional:

        @pl.when(away)
        def _(copy=copy):
            copy.wait_send()

    @pl.when(is_host)
    def _():
        for what in hosted:
            away, copy, _, _ = returned(*what)

            @pl.when(away)
            def _(copy=copy):
                copy.wait_send()

    assert counter[0] <= SEMS


def on_device(q, k, v, grad, codes, index, table, down, up):
    weight = dequantize(codes, index, table)
    vmem = pl.BlockSpec(memory_space=pltpu.VMEM)
    tokens, width = q.shape
    out = jax.ShapeDtypeStruct((tokens, width), bf16)
    slabs = pltpu.VMEM((8, 192, 128), bf16)
    results = pl.pallas_call(
        kernel,
        name="block_backward",
        out_shape=(
            out,
            out,
            out,
            jax.ShapeDtypeStruct((1, width), f32),
            jax.ShapeDtypeStruct((1, grad.shape[1]), f32),
        ),
        in_specs=[vmem] * 7,
        out_specs=[vmem] * 5,
        scratch_shapes=[
            pltpu.VMEM((8, 8, 80, 256), bf16),
            pltpu.VMEM((8, 8, 80, 256), bf16),
            pltpu.VMEM((8, 192, 640), bf16),
            slabs,
            slabs,
            slabs,
            slabs,
            pltpu.VMEM((10, BLOCK, BLOCK), f32),
            pltpu.VMEM((128, 1536), bf16),
            pltpu.VMEM((192, 512), bf16),
            slabs,
            slabs,
            slabs,
            slabs,
            pltpu.VMEM((1536, 128), f32),
            pltpu.VMEM((1536, 128), f32),
            pltpu.VMEM((192, 512), bf16),
            pltpu.VMEM((8, 1, 1152), f32),
            pltpu.VMEM((8, 8, 1152), f32),
            pltpu.VMEM((2, 8, 24, 128), f32),
            pltpu.VMEM((2, 8, 24, 128), f32),
            pltpu.VMEM((2, 8, 24, 128), f32),
            pltpu.VMEM((8, 8, 1152), f32),
            pltpu.VMEM((8, 8, 1152), f32),
            pltpu.VMEM((8, 1, 1152), f32),
            pltpu.VMEM((8, 1, 1152), f32),
            pltpu.SemaphoreType.DMA((SEMS,)),
            pltpu.SemaphoreType.DMA((SEMS,)),
            pltpu.SemaphoreType.DMA((3,)),
        ],
        compiler_params=pltpu.CompilerParams(
            collective_id=0, has_side_effects=True, vmem_limit_bytes=56 * 1024 * 1024
        ),
    )(q, k, v, grad, weight, down, up)
    return results


def solution(mesh):
    spec = P("ctx", "fsdp")
    return jax.shard_map(
        on_device,
        mesh=mesh,
        in_specs=(spec, spec, spec, spec, spec, spec, P(), spec, spec),
        out_specs=(spec,) * 5,
        check_vma=False,
    )
```

time: 580 us -> 117 us (0.20)
  blocking collectives: 245 us -> 0 us
  starting transfers between devices: 182 us -> 0 us
  Pallas kernels: 0 us -> 108 us
  local copies, waits for them, and re-layouts: 61.5 us -> 6.41 us
  matrix products: 45.2 us -> 0 us
  between operations: 15 us -> 0.7 us
  other arithmetic: 14.6 us -> 1.14 us
  waiting for transfers between devices: 12.6 us -> 0 us
    all_gather x1 -> x0, blocking collectives: 185 us -> none  [side_by_side(): result = lax.all_gather(both, axis, axis=dim, tiled=True)]
    ppermute x42 -> x0, starting transfers between devices: 148 us -> none  [passed_along(): return lax.ppermute(block, axis, route)]
    pallas_call x0 -> x1, Pallas kernels: none -> 108 us  [on_device(): pl.pallas_call(kernel, name='block_backward', out_shape=(out, out, out, j...]
    psum x1 -> x0, blocking collectives: 59.5 us -> none  [on_device(): lax.psum(backward_piece, 'fsdp')]
    dot_general x42 -> x0, matrix products: 45.2 us -> none  [the longest x4 8.38 us: far_head(): jnp.dot(far_score_grad.T, query_far, preferred_element_type=jnp.float32)]
    all_to_all x3 -> x0, starting transfers between devices: 34.5 us -> none  [the longest x2 24.1 us: copy_for_each(): return lax.all_to_all(copies, axis, split_axis=0, concat_axis=0, tiled=True)]
    dynamic_slice x12 -> x0, local copies, waits for them, and re-layouts: 12.8 us -> none  [the longest x8 9.56 us: on_device(): lax.map(attend_head, (query_major, keys_major, values_major, grad_major,...]
    ppermute x42 -> x0, waiting for transfers between devices: 12.6 us -> none  [passed_along(): return lax.ppermute(block, axis, route)]
  transfers between devices with their start and end apart: 46 -> 0, of which waited for: 5 -> 0; matrix products, arithmetic and copies ran while one was open for 20% -> 0% of each run, Pallas kernels for 0% -> 0%
where the time goes in v1:
time: 117 us
  Pallas kernels  108 us (92%)
  local copies, waits for them, and re-layouts  6.41 us (5%)
    pallas_call x1, Pallas kernels, on_device(): pl.pallas_call(kernel, name='block_backward', out_shape=(out, out, out, j...  108 us
    unnamed x18, local copies, waits for them, and re-layouts  6.15 us

profile of v1, /device:TPU:1, one launch (start us, length us, event | category | flops | bytes accessed | tf_op | source)
XLA Modules:
  0.0 116.6 jit_solution(17513697050257931089)
XLA Ops:
  0.6 0.0 copy-start.5
  0.6 0.8 copy.16
  1.4 0.0 copy-done.5
  1.4 0.3 select_reduce_fusion
  1.7 0.1 broadcast_in_dim.96
  1.8 0.0 copy-start.2
  1.8 0.1 reshape.14
  2.0 0.8 copy-done.2
  2.8 0.9 multiply_convert_fusion.w_ref
  3.6 108.3 %block_backward.1 = (bf16[192,512]{1,0:T(8,128)(2,1)}, bf16[192,512]{1,0:T(8,128)(2,1)}, bf16[192,512]{1,0:T(8,128)(2,1)}, f32[1,512]{1,0:T(1,128)}, f32[1,640]{1,0:T(1,128)}) custom-call(bf16[192,512]{1,0:T(8,128)(2,1)} %q_ref.1, bf16[192,512]{1,0:T(8,128)(2,1)} %k_ref.1, bf16[192,512]{1,0:T(8,128)(2,1)} %v_ref.1, bf16[192,640]{1,0:T(8,128)(2,1)} %g_ref.1, ...), custom_call_target="tpu_custom_call" | custom-call | tf_op jit(solution)/shard_map/block_backward/pallas_call | solution.py:550
  112.0 0.0 copy-start.1
  112.0 1.7 %copy.22 = bf16[192,512]{1,0:T(8,128)(2,1)} copy(bf16[192,512]{1,0:T(8,128)(2,1)} %get-tuple-element.10) | data formatting | bytes 393216
  113.6 0.0 copy-done.1
  113.6 0.0 copy-start
  113.6 0.7 copy.23
  114.3 0.3 copy-done
  114.6 0.0 copy-start.4
  114.6 0.7 copy.24
  115.3 0.0 copy-done.4
  115.3 0.0 copy-start.3
  115.3 0.6 copy.25
  115.9 0.1 copy-done.3
  116.0 0.6 copy.26
Async XLA Ops:
  0.6 0.8 copy-start.5
  1.8 0.9 copy-start.2
  112.0 1.7 %copy-start.1 = (bf16[192,512]{1,0:T(8,128)(2,1)S(1)}, bf16[192,512]{1,0:T(8,128)(2,1)}, u32[]{:S(2)}) copy-start(bf16[192,512]{1,0:T(8,128)(2,1)} %get-tuple-element.11) | copy-start | bytes 589828
  113.6 1.0 copy-start
  114.6 0.7 copy-start.4
  115.3 0.7 copy-start.3

commit v2 on v1

v2 whole, which is shorter than its diff:
```python
import jax
import jax.numpy as jnp
from jax import lax
from jax.experimental import pallas as pl
from jax.experimental.pallas import tpu as pltpu
from jax.sharding import PartitionSpec as P

HEAD_WIDTH = 128
MESH = pl.DeviceIdType.MESH
BLOCK = 384
nf4_values = (
    -1.0,
    -0.6961928009986877,
    -0.5250730514526367,
    -0.39491748809814453,
    -0.28444138169288635,
    -0.18477343022823334,
    -0.09105003625154495,
    0.0,
    0.07958029955625534,
    0.16093020141124725,
    0.24611230194568634,
    0.33791524171829224,
    0.44070982933044434,
    0.5626170039176941,
    0.7229568362236023,
    1.0,
)
adapter_scale = 0.25
masked = -1e30
f32, bf16 = jnp.float32, jnp.bfloat16
SENDS, RECVS = 24, 64


def nt(a, b):
    return lax.dot_general(a, b, (((1,), (1,)), ((), ())), preferred_element_type=f32)


def tn(a, b):
    return lax.dot_general(a, b, (((0,), (0,)), ((), ())), preferred_element_type=f32)


def nn(a, b):
    return jnp.dot(a, b, preferred_element_type=f32)


def kernel(
    codes_ref, index_ref, table_ref, ad_ref, au_ref, q_ref, k_ref, v_ref, g_ref,
    dq_ref, dk_ref, dv_ref, dn_ref, up_ref,
    WA, WB, GB, QU, KU, VU, DU, PT, KT, OB, OS, DQS, DKS, DVS, DKA, DVA, DOB,
    AD1, AD2, PSS, PSR, PSG, UPD, R1, S2, R2, ss, rs, ls,
):
    ctx = lax.axis_index("ctx")
    f = lax.axis_index("fsdp")
    y, g = ctx // 8, ctx % 8
    x, zl = g // 2, g % 2
    c = f % 2
    partner = f + 1 - 2 * c
    scale = HEAD_WIDTH ** (-0.5)
    is_host = (x % 2) == c
    unit_head = 2 * (x // 2) + zl


    sent, heard = [0], [0]

    def send_id():
        sent[0] += 1
        return sent[0] - 1

    def recv_id():
        heard[0] += 1
        return heard[0] - 1

    def remote(src, dst, send, recv, to_ctx, to_f):
        return pltpu.make_async_remote_copy(
            src_ref=src,
            dst_ref=dst,
            send_sem=ss.at[send],
            recv_sem=rs.at[recv],
            device_id={"ctx": to_ctx, "fsdp": to_f},
            device_id_type=MESH,
        )

    def go(src, send, recv, to_ctx, to_f, dst=None):
        remote(src, src if dst is None else dst, send, recv, to_ctx, to_f).start()

    def arrived(dst, recv):
        pltpu.make_async_copy(dst, dst, rs.at[recv]).wait()

    def left(src, send):
        pltpu.make_async_copy(src, src, ss.at[send]).wait()

    def row(dy):
        return (y + dy) % 8

    def at(yy, gg):
        return yy * 8 + gg

    def ydev(dy):
        return at(row(dy), g)

    def xdev(dx):
        return at(y, ((x + dx) % 4) * 2 + zl)

    def fdev(df):
        return (f + df) % 8

    other_row = jnp.where(x < 2, (y + 7) % 8, (y + 1) % 8)
    other_g = jnp.where(x < 2, 4, 0)

    barrier = pltpu.get_barrier_semaphore()
    peers = [(at(y, (g + j) % 8), f) for j in range(1, 8)]
    peers += [(ydev(j), f) for j in range(1, 8)]
    peers += [(ctx, fdev(j)) for j in range(1, 8)]
    peers += [(at(other_row, other_g + j), f) for j in range(4)]
    for to_ctx, to_f in peers:
        pl.semaphore_signal(
            barrier, inc=1, device_id={"ctx": to_ctx, "fsdp": to_f}, device_id_type=MESH
        )
    own_grad = pltpu.make_async_copy(g_ref, GB.at[f], ls.at[0])
    own_grad.start()

    codes = codes_ref[...]
    values = jnp.zeros(codes.shape, f32)
    for level in range(16):
        values = jnp.where(codes == level, nf4_values[level], values)
    table = table_ref[...]
    level_at = lax.broadcasted_iota(jnp.int32, (codes.shape[0], table.shape[1]), 1)
    block_at = lax.broadcasted_iota(jnp.int32, codes.shape, 1) // 64
    scales = jnp.zeros(codes.shape, f32)
    for block in range(8):
        picked = jnp.where(index_ref[:, block : block + 1] == level_at, table, 0.0)
        picked = jnp.sum(picked, axis=1, keepdims=True)
        scales = jnp.where(block_at == block, picked, scales)
    weight = (values * scales).astype(bf16)
    WA[y, g] = weight[:, :256]
    WB[y, g] = weight[:, 256:]
    AD1[g] = jnp.concatenate([ad_ref[...].astype(f32), au_ref[...].astype(f32)], axis=1)
    pl.semaphore_wait(barrier, len(peers))

    pair = ctx + 1 - 2 * zl
    first, few = recv_id(), send_id()
    go(WA.at[y, g], few, first, pair, f)
    go(WB.at[y, g], few, first, pair, f)

    ad1_s, ad1_r = send_id(), recv_id()
    for j in range(1, 8):
        go(AD1.at[g], ad1_s, ad1_r, at(y, (g + j) % 8), f)

    def PB(dy, dx):
        return WB.at[row(dy), pl.ds(((x + dx) % 4) * 2, 2)]

    def QA(dy, h):
        return WA.at[row(dy), pl.ds(4 * h, 4)]

    up_relay = (-2, -1, 0, 1)
    yb = {d: recv_id() for d in (-4, -3, -2, -1, 1, 2, 3)}
    xlast = recv_id()
    xb = {}
    for d in range(-4, 4):
        xb[(-1, d)] = recv_id() if d in up_relay else xlast
        xb[(1, d)] = xlast if d in up_relay else recv_id()
    all_b, all_a = send_id(), send_id()

    def b_to_x(d):
        go(PB(d, 0), all_b, xb[(-1, d)], xdev(1), f)
        go(PB(d, 0), all_b, xb[(1, d)], xdev(-1), f)

    def b_up(d):
        go(PB(d, 0), all_b, yb[d - 1], ydev(1), f)

    def b_down(d):
        go(PB(d, 0), all_b, yb[d + 1], ydev(-1), f)

    def x_relay(d):
        side = -1 if d in up_relay else 1
        arrived(PB(d, side), xb[(side, d)])
        go(PB(d, side), all_b, xlast, xdev(-side), f)

    ya = {(d, h): recv_id() for d in (-3, -2, -1, 1, 2, 3) for h in (0, 1)}
    ya[(-4, 0)] = recv_id()
    ya[(4, 1)] = recv_id()

    def a_up(d, h):
        go(QA(d, h), all_a, ya[(d - 1, h)], ydev(1), f)

    def a_down(d, h):
        go(QA(d, h), all_a, ya[(d + 1, h)], ydev(-1), f)

    def a_arrived(d, h):
        arrived(QA(d, h), ya[(d, h)])

    def a_step(d, h):
        a_arrived(-d, h)
        if d < 3 or h == 0:
            a_up(-d, h)
        a_arrived(d, h)
        if d < 3 or h == 1:
            a_down(d, h)

    def b_step(d):
        arrived(PB(-d, 0), yb[-d])
        b_up(-d)
        b_to_x(-d)
        arrived(PB(d, 0), yb[d])
        if d < 3:
            b_down(d)
        b_to_x(d)

    arrived(WA.at[0, pl.ds(0, 2)], first)
    b_up(0)
    b_down(0)
    mine = WA.at[y, pl.ds(x * 2, 2)]
    xa = recv_id()
    go(mine, few, xa, xdev(1), f)
    go(mine, few, xa, xdev(-1), f)
    go(mine, all_b, xa, xdev(2), f)
    b_to_x(0)

    half = [pl.ds(0, 96), pl.ds(96, 96)]
    gs = send_id()
    g_own, g_low, g_high, g_low_half, g_high_half, g_rest = [recv_id() for _ in range(6)]
    own_grad.wait()
    go(GB.at[f], gs, g_low, ctx, fdev(2))
    go(GB.at[f], gs, g_high, ctx, fdev(6))
    go(GB.at[f], gs, g_rest, ctx, partner)

    def slab_of(head):
        if head < 2:
            return y, g
        return jnp.where(x < 2, (y + 7) % 8, y), (g + 4) % 8

    def host_of(head):
        yy, _ = slab_of(head)
        return at(yy, (2 * (head // 2) + c) * 2 + head % 2)

    to_host_sends = []

    def to_hosts(src_ref, dst_buf, recv):
        send = send_id()
        to_host_sends.append(send)
        for head in range(4):
            dest = host_of(head)
            _, slot = slab_of(head)
            src = src_ref.at[:, head * 128 : (head + 1) * 128]
            dst = dst_buf.at[slot]
            away = dest != ctx

            @pl.when(away)
            def _():
                go(src, send, recv, dest, f, dst)

            @pl.when(jnp.logical_not(away))
            def _():
                pltpu.make_async_copy(src, dst, rs.at[recv]).start()

    ki, qi, vi, di = [recv_id() for _ in range(4)]
    to_hosts(k_ref, KU, ki)
    to_hosts(q_ref, QU, qi)
    to_hosts(v_ref, VU, vi)

    arrived(AD1.at[pl.ds(0, 7)], ad1_r)
    AD2[y] = jnp.concatenate([AD1[j] for j in range(8)], axis=0)
    ad2_s, ad2_r = send_id(), recv_id()
    for j in range(1, 8):
        go(AD2.at[y], ad2_s, ad2_r, ydev(j), f)

    arrived(WA.at[0, pl.ds(0, 6)], xa)
    a_up(0, 0)
    a_down(0, 0)

    b_step(1)
    x_relay(0)
    a_up(0, 1)
    a_down(0, 1)

    b_step(2)
    x_relay(-1)
    x_relay(1)
    a_step(1, 0)

    below, above, across = fdev(6), fdev(2), fdev(4)
    arrived(GB.at[below], g_low)
    go(GB.at[below, half[0]], gs, g_low_half, ctx, above)
    go(GB.at[below], gs, g_rest, ctx, partner)
    arrived(GB.at[above], g_high)
    go(GB.at[above, half[1]], gs, g_high_half, ctx, below)
    go(GB.at[above], gs, g_rest, ctx, partner)

    def sum_start(n, piece):
        PSS[n] = piece.reshape(8, 24, 128)
        send, recv = send_id(), recv_id()
        for j in range(1, 8):
            to = fdev(j)
            go(PSS.at[n, to], send, recv, ctx, to, PSR.at[n, f])
        return send, recv

    def sum_middle(n, pair, factor):
        arrived(PSR.at[n, pl.ds(0, 7)], pair[1])
        total = PSS[n, f]
        for j in range(1, 8):
            total = total + PSR[n, fdev(j)]
        PSG[n, f] = (total * factor).astype(bf16).astype(f32)
        send, recv = send_id(), recv_id()
        for j in range(1, 8):
            go(PSG.at[n, f], send, recv, ctx, fdev(j))
        return send, recv

    def sum_end(n, pair):
        arrived(PSG.at[n, pl.ds(0, 7)], pair[1])
        return PSG[n].reshape(192, 128).astype(bf16)

    arrived(AD2.at[pl.ds(0, 7)], ad2_r)
    adapters = AD2[...].reshape(64, 1152).astype(bf16)
    adapters = jnp.concatenate([adapters, jnp.zeros_like(adapters)], axis=0)
    down_full, up_piece = adapters[:, :512], adapters[:, 512:]
    back0 = sum_start(0, nt(GB[f], up_piece))

    def source_of(slot):
        if slot < 4:
            return jnp.where(x < 2, at(y, slot), at(y, slot + 4))
        return jnp.where(x < 2, at(y, slot), at(row(1), slot - 4))

    head_columns = pl.ds(pl.multiple_of(unit_head * 128, 128), 128)

    def from_host(buf, dst_ref, send, recv, slot):
        dest = source_of(slot)
        src, dst = buf.at[slot], dst_ref.at[:, head_columns]
        away = dest != ctx

        @pl.when(away)
        def _():
            go(src, send, recv, dest, f, dst)

        @pl.when(jnp.logical_not(away))
        def _():
            pltpu.make_async_copy(src, dst, rs.at[recv]).start()

    blocks = 1536 // BLOCK

    def two(buf, b):
        return buf[2 * b : 2 * b + 2].reshape(BLOCK, 128)

    def tile(b, kb):
        return b * (b + 1) // 2 + kb

    oh, oi = send_id(), recv_id()

    def forward(b):
        key_at = lax.broadcasted_iota(jnp.int32, (BLOCK, BLOCK), 0)
        query_at = lax.broadcasted_iota(jnp.int32, (BLOCK, BLOCK), 1)
        seen = key_at <= query_at
        query = two(QU, b)
        parts = []
        for kb in range(b + 1):
            part = nt(two(KU, kb), query) * scale
            parts.append(jnp.where(seen, part, masked) if kb == b else part)
        top = jnp.max(parts[0], axis=0, keepdims=True)
        for part in parts[1:]:
            top = jnp.maximum(top, jnp.max(part, axis=0, keepdims=True))
        parts = [jnp.exp(part - top) for part in parts]
        total = jnp.sum(parts[0], axis=0, keepdims=True)
        for part in parts[1:]:
            total = total + jnp.sum(part, axis=0, keepdims=True)
        inverse = 1.0 / total
        out = jnp.zeros((BLOCK, 128), f32)
        for kb in range(b + 1):
            prob = parts[kb] * inverse
            PT[tile(b, kb)] = prob
            out = out + tn(prob.astype(bf16), two(VU, kb))
        OS[2 * b : 2 * b + 2] = out.astype(bf16).reshape(2, 192, 128)
        for s in (2 * b, 2 * b + 1):
            from_host(OS, OB, oh, oi, s)

    b_step(3)
    x_relay(-2)
    x_relay(2)
    a_step(1, 1)


    @pl.when(is_host)
    def _():
        arrived(KU, ki)
        arrived(QU, qi)
        arrived(VU, vi)
        for b in (0, 1):
            forward(b)

    arrived(PB(-4, 0), yb[-4])
    b_to_x(-4)
    x_relay(-3)
    x_relay(3)
    a_step(2, 0)


    @pl.when(is_host)
    def _():
        forward(2)

    back0 = (back0, sum_middle(0, back0, adapter_scale))
    x_relay(-4)
    a_step(2, 1)

    @pl.when(is_host)
    def _():
        forward(3)

    arrived(GB.at[across, half[0]], g_low_half)
    go(GB.at[across, half[0]], gs, g_rest, ctx, partner)
    arrived(GB.at[across, half[1]], g_high_half)
    go(GB.at[across, half[1]], gs, g_rest, ctx, partner)

    a_step(3, 0)
    a_step(3, 1)

    arrived(OB, oi)
    mid0 = sum_start(1, nt(OB[...], down_full))
    lora_back = sum_end(0, back0[1])
    UPD[:, :, 0:512] = tn(lora_back, OB[...])[:64].reshape(8, 8, 512)
    total_a = nn(lora_back, down_full[:, :256])
    total_b = nn(lora_back, down_full[:, 256:])

    arrived(GB.at[pl.ds(0, 4)], g_rest)

    def a_part(d):
        yy = row(d)
        return nn(GB[yy], WA[yy].reshape(640, 256))

    mid1 = sum_middle(1, mid0, 1.0)
    for d in (0, -1, 1, -2, 2, -3, 3):
        total_a = total_a + a_part(d)

    lora_mid = sum_end(1, mid1)
    UPD[:, :, 512:1152] = (adapter_scale * tn(lora_mid, GB[f]))[:64].reshape(8, 8, 640)
    rs1_s, rs1_r = send_id(), recv_id()
    for j in range(1, 8):
        go(UPD.at[row(j)], rs1_s, rs1_r, ydev(j), f, R1.at[y])

    a_arrived(-4, 0)
    a_arrived(4, 1)
    total_a = total_a + a_part(4)
    DOB[:, 0:256] = total_a.astype(bf16)

    arrived(WB.at[pl.ds(0, 4)], xlast)
    for yy in range(8):
        total_b = total_b + nn(GB[yy], WB[yy].reshape(640, 256))
    DOB[:, 256:512] = total_b.astype(bf16)
    to_hosts(DOB, DU, di)

    arrived(R1.at[pl.ds(0, 7)], rs1_r)
    total = UPD[y]
    for j in range(1, 8):
        total = total + R1[row(j)]
    for j in range(8):
        S2[j] = total[j : j + 1]
    rs2_s, rs2_r = send_id(), recv_id()
    for j in range(1, 8):
        to = (g + j) % 8
        go(S2.at[to], rs2_s, rs2_r, at(y, to), f, R2.at[g])

    gq, gk, gv = [recv_id() for _ in range(3)]
    hq, hk, hv = [send_id() for _ in range(3)]


    @pl.when(is_host)
    def _():
        for kb in range(blocks):
            KT[:, kb * BLOCK : (kb + 1) * BLOCK] = two(KU, kb).astype(f32).T.astype(bf16)
        DKA[...] = jnp.zeros_like(DKA)
        DVA[...] = jnp.zeros_like(DVA)
        arrived(DU, di)
        for b in reversed(range(blocks)):
            grad, query = two(DU, b), two(QU, b)
            parts = []
            delta = jnp.zeros((1, BLOCK), f32)
            for kb in range(b + 1):
                part = nt(two(VU, kb), grad)
                delta = delta + jnp.sum(PT[tile(b, kb)] * part, axis=0, keepdims=True)
                parts.append(part)
            turned = jnp.zeros((128, BLOCK), f32)
            for kb in range(b + 1):
                span = pl.ds(kb * BLOCK, BLOCK)
                prob = PT[tile(b, kb)]
                pull = (prob * (parts[kb] - delta) * scale).astype(bf16)
                DKA[span] += nn(pull, query)
                DVA[span] += nn(prob.astype(bf16), grad)
                turned = turned + nn(KT[:, span], pull)
            span = pl.ds(b * BLOCK, BLOCK)
            DQS[2 * b : 2 * b + 2] = turned.T.astype(bf16).reshape(2, 192, 128)
            DKS[2 * b : 2 * b + 2] = DKA[span].astype(bf16).reshape(2, 192, 128)
            DVS[2 * b : 2 * b + 2] = DVA[span].astype(bf16).reshape(2, 192, 128)
            for s in (2 * b, 2 * b + 1):
                from_host(DQS, dq_ref, hq, gq, s)
                from_host(DKS, dk_ref, hk, gk, s)
                from_host(DVS, dv_ref, hv, gv, s)

    arrived(R2.at[pl.ds(0, 7)], rs2_r)
    total = S2[g]
    for j in range(1, 8):
        total = total + R2[(g + j) % 8]
    dn_ref[...] = total[:, 0:512]
    up_ref[...] = total[:, 512:1152]

    arrived(dq_ref, gq)
    arrived(dk_ref, gk)
    arrived(dv_ref, gv)

    seven = pl.ds(0, 7)
    left(WA.at[0, pl.ds(0, 6)], few)
    left(WB, all_b)
    left(WA.at[seven], all_a)
    left(GB.at[seven], gs)
    left(AD1.at[seven], ad1_s)
    left(AD2.at[seven], ad2_s)
    left(PSS.at[0, seven], back0[0][0])
    left(PSG.at[0, seven], back0[1][0])
    left(PSS.at[1, seven], mid0[0])
    left(PSG.at[1, seven], mid1[0])
    left(UPD.at[seven], rs1_s)
    left(S2.at[seven], rs2_s)

    @pl.when(is_host)
    def _():
        for send in to_host_sends:
            left(KU.at[pl.ds(0, 3)], send)
        for send in (oh, hq, hk, hv):
            left(OS.at[seven], send)

    @pl.when(jnp.logical_not(is_host))
    def _():
        for send in to_host_sends:
            left(KU.at[pl.ds(0, 4)], send)

    assert sent[0] <= SENDS and heard[0] <= RECVS, (sent, heard)


def finish_kernel(*refs):
    for src, dst in zip(refs[:5], refs[5:]):
        dst[...] = src[...]


def on_device(q, k, v, grad, codes, index, table, down, up):
    vmem = pl.BlockSpec(memory_space=pltpu.VMEM)
    tokens, width = q.shape
    out = jax.ShapeDtypeStruct((tokens, width), bf16)
    slabs = pltpu.VMEM((8, 192, 128), bf16)
    results = pl.pallas_call(
        kernel,
        name="block_backward",
        out_shape=(
            out,
            out,
            out,
            jax.ShapeDtypeStruct((1, width), f32),
            jax.ShapeDtypeStruct((1, grad.shape[1]), f32),
        ),
        in_specs=[vmem] * 5 + [pl.BlockSpec(memory_space=pl.ANY)] * 4,
        out_specs=[vmem] * 5,
        scratch_shapes=[
            pltpu.VMEM((8, 8, 80, 256), bf16),
            pltpu.VMEM((8, 8, 80, 256), bf16),
            pltpu.VMEM((8, 192, 640), bf16),
            slabs,
            slabs,
            slabs,
            slabs,
            pltpu.VMEM((10, BLOCK, BLOCK), f32),
            pltpu.VMEM((128, 1536), bf16),
            pltpu.VMEM((192, 512), bf16),
            slabs,
            slabs,
            slabs,
            slabs,
            pltpu.VMEM((1536, 128), f32),
            pltpu.VMEM((1536, 128), f32),
            pltpu.VMEM((192, 512), bf16),
            pltpu.VMEM((8, 1, 1152), f32),
            pltpu.VMEM((8, 8, 1152), f32),
            pltpu.VMEM((2, 8, 24, 128), f32),
            pltpu.VMEM((2, 8, 24, 128), f32),
            pltpu.VMEM((2, 8, 24, 128), f32),
            pltpu.VMEM((8, 8, 1152), f32),
            pltpu.VMEM((8, 8, 1152), f32),
            pltpu.VMEM((8, 1, 1152), f32),
            pltpu.VMEM((8, 1, 1152), f32),
            pltpu.SemaphoreType.DMA((SENDS,)),
            pltpu.SemaphoreType.DMA((RECVS,)),
            pltpu.SemaphoreType.DMA((1,)),
        ],
        compiler_params=pltpu.CompilerParams(
            collective_id=0, has_side_effects=True, vmem_limit_bytes=56 * 1024 * 1024
        ),
    )(codes, index, table.reshape(1, -1), down, up, q, k, v, grad)
    return pl.pallas_call(
        finish_kernel,
        name="finish",
        out_shape=tuple(jax.ShapeDtypeStruct(r.shape, r.dtype) for r in results),
        in_specs=[vmem] * 5,
        out_specs=[vmem] * 5,
    )(*results)


def solution(mesh):
    spec = P("ctx", "fsdp")
    return jax.shard_map(
        on_device,
        mesh=mesh,
        in_specs=(spec, spec, spec, spec, spec, spec, P(), spec, spec),
        out_specs=(spec,) * 5,
        check_vma=False,
    )
```

time: 117 us -> 104 us (0.89)
  Pallas kernels: 108 us -> 101 us
  local copies, waits for them, and re-layouts: 6.41 us -> 1.39 us
    pallas_call x1, Pallas kernels: 108 us -> 99 us  [on_device(): pl.pallas_call(kernel, name='block_backward', out_shape=(out, out, out, j...]
    unnamed x18 -> x1, local copies, waits for them, and re-layouts: 6.15 us -> 1.39 us
    pallas_call x0 -> x1, Pallas kernels: none -> 1.95 us  [on_device(): pl.pallas_call(finish_kernel, name='finish', out_shape=tuple((jax.ShapeDt...]
where the time goes in v2:
time: 104 us; the launch traced here: 103 us
  Pallas kernels  101 us (97%)
  local copies, waits for them, and re-layouts  1.39 us (1%)
    pallas_call x1, Pallas kernels, on_device(): pl.pallas_call(kernel, name='block_backward', out_shape=(out, out, out, j...  99 us

profile of v2, /device:TPU:1, one launch (start us, length us, event | category | flops | bytes accessed | tf_op | source)
XLA Modules:
  0.0 103.0 jit_solution(15933203588188702733)
XLA Ops:
  0.6 1.4 %copy.14.index_ref = s32[80,8]{1,0:T(8,128)} copy(s32[80,8]{0,1:T(8,128)} %param.14) | data formatting | bytes 5120 | tf_op args[5]
  2.0 99.0 %block_backward.1 = (bf16[192,512]{1,0:T(8,128)(2,1)}, bf16[192,512]{1,0:T(8,128)(2,1)}, bf16[192,512]{1,0:T(8,128)(2,1)}, f32[1,512]{1,0:T(1,128)}, f32[1,640]{1,0:T(1,128)}) custom-call(s32[80,512]{1,0:T(8,128)} %codes_ref.1, s32[80,8]{1,0:T(8,128)} %copy.14.index_ref, f32[1,256]{1,0:T(1,128)} %bitcast.1, bf16[1,512]{1,0:T(2,128)(2,1)} %ad_ref.1, ...), custom_call_target="tpu_custom_call" | custom-call | tf_op jit(solution)/shard_map/block_backward/pallas_call | solution.py:547
  101.0 2.0 %finish.1 = (bf16[192,512]{1,0:T(8,128)(2,1)}, bf16[192,512]{1,0:T(8,128)(2,1)}, bf16[192,512]{1,0:T(8,128)(2,1)}, f32[1,512]{1,0:T(1,128)}, f32[1,640]{1,0:T(1,128)}) custom-call(bf16[192,512]{1,0:T(8,128)(2,1)} %get-tuple-element.10.refs_0_, bf16[192,512]{1,0:T(8,128)(2,1)} %get-tuple-element.11.refs_1_, bf16[192,512]{1,0:T(8,128)(2,1)} %get-tuple-element.12.refs_2_, ...), custom_call_target="tpu_custom_call" | custom-call | tf_op jit(solution)/shard_map/finish/pallas_call | solution.py:594

commit v3 on v2

--- a/solution.py
+++ b/solution.py
@@ -57,8 +57,10 @@
     c = f % 2
     partner = f + 1 - 2 * c
     scale = HEAD_WIDTH ** (-0.5)
-    is_host = (x % 2) == c
-    unit_head = 2 * (x // 2) + zl
+    shifted_x = 3 * (1 - c)
+    shifted_host = x == shifted_x
+    is_host = jnp.logical_or(x == 1 + c, shifted_host)
+    unit_head = jnp.where(shifted_host, 2, 0) + zl
 
 
     sent, heard = [0], [0]
@@ -125,11 +127,13 @@
     for level in range(16):
         values = jnp.where(codes == level, nf4_values[level], values)
     table = table_ref[...]
+    index = jnp.concatenate([index_ref[...].astype(f32), jnp.zeros((8, 48), f32)], axis=1)
+    index = index.T[: codes.shape[0]].astype(jnp.int32)
     level_at = lax.broadcasted_iota(jnp.int32, (codes.shape[0], table.shape[1]), 1)
     block_at = lax.broadcasted_iota(jnp.int32, codes.shape, 1) // 64
     scales = jnp.zeros(codes.shape, f32)
     for block in range(8):
-        picked = jnp.where(index_ref[:, block : block + 1] == level_at, table, 0.0)
+        picked = jnp.where(index[:, block : block + 1] == level_at, table, 0.0)
         picked = jnp.sum(picked, axis=1, keepdims=True)
         scales = jnp.where(block_at == block, picked, scales)
     weight = (values * scales).astype(bf16)
@@ -226,22 +230,20 @@
     go(GB.at[f], gs, g_rest, ctx, partner)
 
     def slab_of(head):
+        return g if head < 2 else (g + 4) % 8
+
+    def host_of(head):
         if head < 2:
-            return y, g
-        return jnp.where(x < 2, (y + 7) % 8, y), (g + 4) % 8
-
-    def host_of(head):
-        yy, _ = slab_of(head)
-        return at(yy, (2 * (head // 2) + c) * 2 + head % 2)
+            return at(y, (1 + c) * 2 + head)
+        first_row = jnp.where(x < 2, (y + 7) % 8, y)
+        return at((first_row + c) % 8, shifted_x * 2 + head - 2)
 
     to_host_sends = []
 
-    def to_hosts(src_ref, dst_buf, recv):
-        send = send_id()
-        to_host_sends.append(send)
-        for head in range(4):
+    def to_hosts(src_ref, dst_buf, recv, send, heads):
+        for head in heads:
             dest = host_of(head)
-            _, slot = slab_of(head)
+            slot = slab_of(head)
             src = src_ref.at[:, head * 128 : (head + 1) * 128]
             dst = dst_buf.at[slot]
             away = dest != ctx
@@ -255,21 +257,25 @@
                 pltpu.make_async_copy(src, dst, rs.at[recv]).start()
 
     ki, qi, vi, di = [recv_id() for _ in range(4)]
-    to_hosts(k_ref, KU, ki)
-    to_hosts(q_ref, QU, qi)
-    to_hosts(v_ref, VU, vi)
-
+    ks, qs, vs, ds = to_host_sends = [send_id() for _ in range(4)]
+
+    def slabs():
+        to_hosts(k_ref, KU, ki, ks, range(4))
+        to_hosts(q_ref, QU, qi, qs, range(4))
+        to_hosts(v_ref, VU, vi, vs, range(4))
+
+    b_step(1)
+    arrived(WA.at[0, pl.ds(0, 6)], xa)
+    a_up(0, 0)
+    a_down(0, 0)
+
+    slabs()
     arrived(AD1.at[pl.ds(0, 7)], ad1_r)
     AD2[y] = jnp.concatenate([AD1[j] for j in range(8)], axis=0)
     ad2_s, ad2_r = send_id(), recv_id()
     for j in range(1, 8):
         go(AD2.at[y], ad2_s, ad2_r, ydev(j), f)
 
-    arrived(WA.at[0, pl.ds(0, 6)], xa)
-    a_up(0, 0)
-    a_down(0, 0)
-
-    b_step(1)
     x_relay(0)
     a_up(0, 1)
     a_down(0, 1)
@@ -316,10 +322,12 @@
     down_full, up_piece = adapters[:, :512], adapters[:, 512:]
     back0 = sum_start(0, nt(GB[f], up_piece))
 
+    first_row = (y + 8 - c) % 8
+
     def source_of(slot):
         if slot < 4:
-            return jnp.where(x < 2, at(y, slot), at(y, slot + 4))
-        return jnp.where(x < 2, at(y, slot), at(row(1), slot - 4))
+            return jnp.where(shifted_host, at(first_row, slot + 4), at(y, slot))
+        return jnp.where(shifted_host, at((first_row + 1) % 8, slot - 4), at(y, slot))
 
     head_columns = pl.ds(pl.multiple_of(unit_head * 128, 128), 128)
 
@@ -383,6 +391,8 @@
         arrived(KU, ki)
         arrived(QU, qi)
         arrived(VU, vi)
+        for kb in range(blocks):
+            KT[:, kb * BLOCK : (kb + 1) * BLOCK] = two(KU, kb).astype(f32).T.astype(bf16)
         for b in (0, 1):
             forward(b)
 
@@ -413,22 +423,73 @@
     a_step(3, 0)
     a_step(3, 1)
 
+    arrived(GB.at[pl.ds(0, 4)], g_rest)
+
+    def a_part(d):
+        yy = row(d)
+        return nn(GB[yy], WA[yy].reshape(640, 256))
+
+    total_a = a_part(0)
+    for d in (-1, 1, -2, 2, -3, 3):
+        total_a = total_a + a_part(d)
     arrived(OB, oi)
     mid0 = sum_start(1, nt(OB[...], down_full))
     lora_back = sum_end(0, back0[1])
     UPD[:, :, 0:512] = tn(lora_back, OB[...])[:64].reshape(8, 8, 512)
-    total_a = nn(lora_back, down_full[:, :256])
+    total_a = total_a + nn(lora_back, down_full[:, :256])
     total_b = nn(lora_back, down_full[:, 256:])
 
-    arrived(GB.at[pl.ds(0, 4)], g_rest)
-
-    def a_part(d):
-        yy = row(d)
-        return nn(GB[yy], WA[yy].reshape(640, 256))
+
+    a_arrived(-4, 0)
+    a_arrived(4, 1)
+    total_a = total_a + a_part(4)
+    DOB[:, 0:256] = total_a.astype(bf16)
+    to_hosts(DOB, DU, di, ds, (0, 1))
+
+    arrived(WB.at[pl.ds(0, 4)], xlast)
+    for yy in range(8):
+        total_b = total_b + nn(GB[yy], WB[yy].reshape(640, 256))
+    DOB[:, 256:512] = total_b.astype(bf16)
+    to_hosts(DOB, DU, di, ds, (2, 3))
+
+    gq, gk, gv = [recv_id() for _ in range(3)]
+    hq, hk, hv = [send_id() for _ in range(3)]
+
+    def backward(b):
+        grad, query = two(DU, b), two(QU, b)
+        parts = []
+        delta = jnp.zeros((1, BLOCK), f32)
+        for kb in range(b + 1):
+            part = nt(two(VU, kb), grad)
+            delta = delta + jnp.sum(PT[tile(b, kb)] * part, axis=0, keepdims=True)
+            parts.append(part)
+        turned = jnp.zeros((128, BLOCK), f32)
+        for kb in reversed(range(b + 1)):
+            span = pl.ds(kb * BLOCK, BLOCK)
+            prob = PT[tile(b, kb)]
+            pull = (prob * (parts[kb] - delta) * scale).astype(bf16)
+            key_part, value_part = nn(pull, query), nn(prob.astype(bf16), grad)
+            if b < blocks - 1:
+                key_part, value_part = DKA[span] + key_part, DVA[span] + value_part
+            if kb == b:
+                DKS[2 * b : 2 * b + 2] = key_part.astype(bf16).reshape(2, 192, 128)
+                DVS[2 * b : 2 * b + 2] = value_part.astype(bf16).reshape(2, 192, 128)
+                for s in (2 * b, 2 * b + 1):
+                    from_host(DKS, dk_ref, hk, gk, s)
+                    from_host(DVS, dv_ref, hv, gv, s)
+            else:
+                DKA[span], DVA[span] = key_part, value_part
+            turned = turned + nn(KT[:, span], pull)
+        DQS[2 * b : 2 * b + 2] = turned.T.astype(bf16).reshape(2, 192, 128)
+        for s in (2 * b, 2 * b + 1):
+            from_host(DQS, dq_ref, hq, gq, s)
 
     mid1 = sum_middle(1, mid0, 1.0)
-    for d in (0, -1, 1, -2, 2, -3, 3):
-        total_a = total_a + a_part(d)
+
+    @pl.when(is_host)
+    def _():
+        arrived(DU, di)
+        backward(3)
 
     lora_mid = sum_end(1, mid1)
     UPD[:, :, 512:1152] = (adapter_scale * tn(lora_mid, GB[f]))[:64].reshape(8, 8, 640)
@@ -436,16 +497,10 @@
     for j in range(1, 8):
         go(UPD.at[row(j)], rs1_s, rs1_r, ydev(j), f, R1.at[y])
 
-    a_arrived(-4, 0)
-    a_arrived(4, 1)
-    total_a = total_a + a_part(4)
-    DOB[:, 0:256] = total_a.astype(bf16)
-
-    arrived(WB.at[pl.ds(0, 4)], xlast)
-    for yy in range(8):
-        total_b = total_b + nn(GB[yy], WB[yy].reshape(640, 256))
-    DOB[:, 256:512] = total_b.astype(bf16)
-    to_hosts(DOB, DU, di)
+
+    @pl.when(is_host)
+    def _():
+        backward(2)
 
     arrived(R1.at[pl.ds(0, 7)], rs1_r)
     total = UPD[y]
@@ -458,41 +513,11 @@
         to = (g + j) % 8
         go(S2.at[to], rs2_s, rs2_r, at(y, to), f, R2.at[g])
 
-    gq, gk, gv = [recv_id() for _ in range(3)]
-    hq, hk, hv = [send_id() for _ in range(3)]
-
 
     @pl.when(is_host)
     def _():
-        for kb in range(blocks):
-            KT[:, kb * BLOCK : (kb + 1) * BLOCK] = two(KU, kb).astype(f32).T.astype(bf16)
-        DKA[...] = jnp.zeros_like(DKA)
-        DVA[...] = jnp.zeros_like(DVA)
-        arrived(DU, di)
-        for b in reversed(range(blocks)):
-            grad, query = two(DU, b), two(QU, b)
-            parts = []
-            delta = jnp.zeros((1, BLOCK), f32)
-            for kb in range(b + 1):
-                part = nt(two(VU, kb), grad)
-                delta = delta + jnp.sum(PT[tile(b, kb)] * part, axis=0, keepdims=True)
-                parts.append(part)
-            turned = jnp.zeros((128, BLOCK), f32)
-            for kb in range(b + 1):
-                span = pl.ds(kb * BLOCK, BLOCK)
-                prob = PT[tile(b, kb)]
-                pull = (prob * (parts[kb] - delta) * scale).astype(bf16)
-                DKA[span] += nn(pull, query)
-                DVA[span] += nn(prob.astype(bf16), grad)
-                turned = turned + nn(KT[:, span], pull)
-            span = pl.ds(b * BLOCK, BLOCK)
-            DQS[2 * b : 2 * b + 2] = turned.T.astype(bf16).reshape(2, 192, 128)
-            DKS[2 * b : 2 * b + 2] = DKA[span].astype(bf16).reshape(2, 192, 128)
-            DVS[2 * b : 2 * b + 2] = DVA[span].astype(bf16).reshape(2, 192, 128)
-            for s in (2 * b, 2 * b + 1):
-                from_host(DQS, dq_ref, hq, gq, s)
-                from_host(DKS, dk_ref, hk, gk, s)
-                from_host(DVS, dv_ref, hv, gv, s)
+        for b in (1, 0):
+            backward(b)
 
     arrived(R2.at[pl.ds(0, 7)], rs2_r)
     total = S2[g]
@@ -590,7 +615,7 @@
         compiler_params=pltpu.CompilerParams(
             collective_id=0, has_side_effects=True, vmem_limit_bytes=56 * 1024 * 1024
         ),
-    )(codes, index, table.reshape(1, -1), down, up, q, k, v, grad)
+    )(codes, index.T, table.reshape(1, -1), down, up, q, k, v, grad)
     return pl.pallas_call(
         finish_kernel,
         name="finish",

time: 104 us -> 98.2 us (0.944)
  Pallas kernels: 101 us -> 97.4 us
  local copies, waits for them, and re-layouts: 1.39 us -> 0 us
    pallas_call x1, Pallas kernels: 99 us -> 95.5 us  [on_device(): pl.pallas_call(kernel, name='block_backward', out_shape=(out, out, out, j...]
    unnamed x1 -> x0, local copies, waits for them, and re-layouts: 1.39 us -> none
where the time goes in v3:
time: 98.2 us; the launch traced here: 98.1 us
  Pallas kernels  97.4 us (99%)
    pallas_call x1, Pallas kernels, on_device(): pl.pallas_call(kernel, name='block_backward', out_shape=(out, out, out, j...  95.5 us

profile of v3, /device:TPU:1, one launch (start us, length us, event | category | flops | bytes accessed | tf_op | source)
XLA Modules:
  0.0 98.1 jit_solution(5829326432597278720)
XLA Ops:
  0.6 95.5 %block_backward.1 = (bf16[192,512]{1,0:T(8,128)(2,1)}, bf16[192,512]{1,0:T(8,128)(2,1)}, bf16[192,512]{1,0:T(8,128)(2,1)}, f32[1,512]{1,0:T(1,128)}, f32[1,640]{1,0:T(1,128)}) custom-call(s32[80,512]{1,0:T(8,128)} %codes_ref.1, s32[8,80]{1,0:T(8,128)} %bitcast.2, f32[1,256]{1,0:T(1,128)} %bitcast.3, bf16[1,512]{1,0:T(2,128)(2,1)} %ad_ref.1, ...), custom_call_target="tpu_custom_call" | custom-call | tf_op jit(solution)/shard_map/block_backward/pallas_call | solution.py:572
  96.1 2.0 %finish.1 = (bf16[192,512]{1,0:T(8,128)(2,1)}, bf16[192,512]{1,0:T(8,128)(2,1)}, bf16[192,512]{1,0:T(8,128)(2,1)}, f32[1,512]{1,0:T(1,128)}, f32[1,640]{1,0:T(1,128)}) custom-call(bf16[192,512]{1,0:T(8,128)(2,1)} %get-tuple-element.10.refs_0_, bf16[192,512]{1,0:T(8,128)(2,1)} %get-tuple-element.11.refs_1_, bf16[192,512]{1,0:T(8,128)(2,1)} %get-tuple-element.12.refs_2_, ...), custom_call_target="tpu_custom_call" | custom-call | tf_op jit(solution)/shard_map/finish/pallas_call | solution.py:619

commit v4 on v3

--- a/solution.py
+++ b/solution.py
@@ -29,7 +29,7 @@
 adapter_scale = 0.25
 masked = -1e30
 f32, bf16 = jnp.float32, jnp.bfloat16
-SENDS, RECVS = 24, 64
+SENDS, RECVS = 24, 72
 
 
 def nt(a, b):
@@ -45,10 +45,10 @@
 
 
 def kernel(
-    codes_ref, index_ref, table_ref, ad_ref, au_ref, q_ref, k_ref, v_ref, g_ref,
+    codes_hbm, index_hbm, table_hbm, ad_hbm, au_hbm, q_ref, k_ref, v_ref, g_ref,
     dq_ref, dk_ref, dv_ref, dn_ref, up_ref,
     WA, WB, GB, QU, KU, VU, DU, PT, KT, OB, OS, DQS, DKS, DVS, DKA, DVA, DOB,
-    AD1, AD2, PSS, PSR, PSG, UPD, R1, S2, R2, ss, rs, ls,
+    AD1, AD2, PSS, PSR, PSG, UPD, R1, S2, R2, CODES, INDEX, TABLE, DOWN, UP, ss, rs, ls,
 ):
     ctx = lax.axis_index("ctx")
     f = lax.axis_index("fsdp")
@@ -120,14 +120,30 @@
             barrier, inc=1, device_id={"ctx": to_ctx, "fsdp": to_f}, device_id_type=MESH
         )
     own_grad = pltpu.make_async_copy(g_ref, GB.at[f], ls.at[0])
+    loads = [
+        pltpu.make_async_copy(src, dst, ls.at[n + 1])
+        for n, (src, dst) in enumerate(
+            (
+                (codes_hbm, CODES),
+                (index_hbm, INDEX),
+                (table_hbm, TABLE),
+                (ad_hbm, DOWN),
+                (au_hbm, UP),
+            )
+        )
+    ]
+    for copy in loads:
+        copy.start()
     own_grad.start()
-
-    codes = codes_ref[...]
+    for copy in loads:
+        copy.wait()
+
+    codes = CODES[...]
     values = jnp.zeros(codes.shape, f32)
     for level in range(16):
         values = jnp.where(codes == level, nf4_values[level], values)
-    table = table_ref[...]
-    index = jnp.concatenate([index_ref[...].astype(f32), jnp.zeros((8, 48), f32)], axis=1)
+    table = TABLE[...]
+    index = jnp.concatenate([INDEX[...].astype(f32), jnp.zeros((8, 48), f32)], axis=1)
     index = index.T[: codes.shape[0]].astype(jnp.int32)
     level_at = lax.broadcasted_iota(jnp.int32, (codes.shape[0], table.shape[1]), 1)
     block_at = lax.broadcasted_iota(jnp.int32, codes.shape, 1) // 64
@@ -139,7 +155,7 @@
     weight = (values * scales).astype(bf16)
     WA[y, g] = weight[:, :256]
     WB[y, g] = weight[:, 256:]
-    AD1[g] = jnp.concatenate([ad_ref[...].astype(f32), au_ref[...].astype(f32)], axis=1)
+    AD1[y] = jnp.concatenate([DOWN[...].astype(f32), UP[...].astype(f32)], axis=1)
     pl.semaphore_wait(barrier, len(peers))
 
     pair = ctx + 1 - 2 * zl
@@ -149,15 +165,15 @@
 
     ad1_s, ad1_r = send_id(), recv_id()
     for j in range(1, 8):
-        go(AD1.at[g], ad1_s, ad1_r, at(y, (g + j) % 8), f)
+        go(AD1.at[y], ad1_s, ad1_r, ydev(j), f)
 
     def PB(dy, dx):
         return WB.at[row(dy), pl.ds(((x + dx) % 4) * 2, 2)]
 
-    def QA(dy, h):
-        return WA.at[row(dy), pl.ds(4 * h, 4)]
-
-    up_relay = (-2, -1, 0, 1)
+    def QA(dy, dx):
+        return WA.at[row(dy), pl.ds(((x + dx) % 4) * 2, 2)]
+
+    up_relay = (-1, 0, 1)
     yb = {d: recv_id() for d in (-4, -3, -2, -1, 1, 2, 3)}
     xlast = recv_id()
     xb = {}
@@ -181,26 +197,27 @@
         arrived(PB(d, side), xb[(side, d)])
         go(PB(d, side), all_b, xlast, xdev(-side), f)
 
-    ya = {(d, h): recv_id() for d in (-3, -2, -1, 1, 2, 3) for h in (0, 1)}
-    ya[(-4, 0)] = recv_id()
-    ya[(4, 1)] = recv_id()
-
-    def a_up(d, h):
-        go(QA(d, h), all_a, ya[(d - 1, h)], ydev(1), f)
-
-    def a_down(d, h):
-        go(QA(d, h), all_a, ya[(d + 1, h)], ydev(-1), f)
-
-    def a_arrived(d, h):
-        arrived(QA(d, h), ya[(d, h)])
-
-    def a_step(d, h):
-        a_arrived(-d, h)
-        if d < 3 or h == 0:
-            a_up(-d, h)
-        a_arrived(d, h)
-        if d < 3 or h == 1:
-            a_down(d, h)
+    around = (0, -1, 1, 2)
+    ya = {(d, dx): recv_id() for d in (-3, -2, -1, 1, 2, 3) for dx in around}
+    for d, dx in ((-4, 0), (-4, -1), (4, 1), (4, 2)):
+        ya[(d, dx)] = recv_id()
+
+    def a_up(d, dx):
+        go(QA(d, dx), all_a, ya[(d - 1, dx)], ydev(1), f)
+
+    def a_down(d, dx):
+        go(QA(d, dx), all_a, ya[(d + 1, dx)], ydev(-1), f)
+
+    def a_arrived(d, dx):
+        arrived(QA(d, dx), ya[(d, dx)])
+
+    def a_step(d, dx):
+        a_arrived(-d, dx)
+        if d < 3 or dx in (0, -1):
+            a_up(-d, dx)
+        a_arrived(d, dx)
+        if d < 3 or dx in (1, 2):
+            a_down(d, dx)
 
     def b_step(d):
         arrived(PB(-d, 0), yb[-d])
@@ -211,15 +228,19 @@
             b_down(d)
         b_to_x(d)
 
+    xa = {dx: recv_id() for dx in (-1, 1, 2)}
+
+    def spread(z):
+        block_a, block_b = WA.at[y, 2 * x + z], WB.at[y, 2 * x + z]
+        for up in (1, -1):
+            go(block_b, all_b, yb[-up], ydev(up), f)
+            go(block_a, few, xa[-up], xdev(up), f)
+            go(block_b, all_b, xb[(-up, 0)], xdev(up), f)
+            go(block_a, all_a, ya[(-up, 0)], ydev(up), f)
+
+    spread(zl)
     arrived(WA.at[0, pl.ds(0, 2)], first)
-    b_up(0)
-    b_down(0)
-    mine = WA.at[y, pl.ds(x * 2, 2)]
-    xa = recv_id()
-    go(mine, few, xa, xdev(1), f)
-    go(mine, few, xa, xdev(-1), f)
-    go(mine, all_b, xa, xdev(2), f)
-    b_to_x(0)
+    spread(1 - zl)
 
     half = [pl.ds(0, 96), pl.ds(96, 96)]
     gs = send_id()
@@ -264,64 +285,31 @@
         to_hosts(q_ref, QU, qi, qs, range(4))
         to_hosts(v_ref, VU, vi, vs, range(4))
 
+    for dx in (-1, 1):
+        arrived(QA(0, dx), xa[dx])
+        if dx == -1:
+            part = WA.at[y, ((x + 3) % 4) * 2]
+            go(part, all_b, xa[2], xdev(1), f)
+        else:
+            part = WA.at[y, ((x + 1) % 4) * 2 + 1]
+            go(part, all_b, xa[2], xdev(-1), f)
     b_step(1)
-    arrived(WA.at[0, pl.ds(0, 6)], xa)
-    a_up(0, 0)
-    a_down(0, 0)
-
+    for dx in (-1, 1):
+        a_up(0, dx)
+        a_down(0, dx)
     slabs()
     arrived(AD1.at[pl.ds(0, 7)], ad1_r)
-    AD2[y] = jnp.concatenate([AD1[j] for j in range(8)], axis=0)
+    AD2[g] = jnp.concatenate([AD1[j] for j in range(8)], axis=0).astype(bf16)
     ad2_s, ad2_r = send_id(), recv_id()
     for j in range(1, 8):
-        go(AD2.at[y], ad2_s, ad2_r, ydev(j), f)
-
-    x_relay(0)
-    a_up(0, 1)
-    a_down(0, 1)
-
+        go(AD2.at[g], ad2_s, ad2_r, at(y, (g + j) % 8), f)
+
+    arrived(QA(0, 2), xa[2])
+    a_up(0, 2)
+    a_down(0, 2)
     b_step(2)
-    x_relay(-1)
-    x_relay(1)
     a_step(1, 0)
-
-    below, above, across = fdev(6), fdev(2), fdev(4)
-    arrived(GB.at[below], g_low)
-    go(GB.at[below, half[0]], gs, g_low_half, ctx, above)
-    go(GB.at[below], gs, g_rest, ctx, partner)
-    arrived(GB.at[above], g_high)
-    go(GB.at[above, half[1]], gs, g_high_half, ctx, below)
-    go(GB.at[above], gs, g_rest, ctx, partner)
-
-    def sum_start(n, piece):
-        PSS[n] = piece.reshape(8, 24, 128)
-        send, recv = send_id(), recv_id()
-        for j in range(1, 8):
-            to = fdev(j)
-            go(PSS.at[n, to], send, recv, ctx, to, PSR.at[n, f])
-        return send, recv
-
-    def sum_middle(n, pair, factor):
-        arrived(PSR.at[n, pl.ds(0, 7)], pair[1])
-        total = PSS[n, f]
-        for j in range(1, 8):
-            total = total + PSR[n, fdev(j)]
-        PSG[n, f] = (total * factor).astype(bf16).astype(f32)
-        send, recv = send_id(), recv_id()
-        for j in range(1, 8):
-            go(PSG.at[n, f], send, recv, ctx, fdev(j))
-        return send, recv
-
-    def sum_end(n, pair):
-        arrived(PSG.at[n, pl.ds(0, 7)], pair[1])
-        return PSG[n].reshape(192, 128).astype(bf16)
-
-    arrived(AD2.at[pl.ds(0, 7)], ad2_r)
-    adapters = AD2[...].reshape(64, 1152).astype(bf16)
-    adapters = jnp.concatenate([adapters, jnp.zeros_like(adapters)], axis=0)
-    down_full, up_piece = adapters[:, :512], adapters[:, 512:]
-    back0 = sum_start(0, nt(GB[f], up_piece))
-
+    a_step(1, -1)
     first_row = (y + 8 - c) % 8
 
     def source_of(slot):
@@ -380,10 +368,41 @@
         for s in (2 * b, 2 * b + 1):
             from_host(OS, OB, oh, oi, s)
 
+    def sum_start(n, piece):
+        PSS[n] = piece.reshape(8, 24, 128)
+        send, recv = send_id(), recv_id()
+        for j in range(1, 8):
+            to = fdev(j)
+            go(PSS.at[n, to], send, recv, ctx, to, PSR.at[n, f])
+        return send, recv
+
+    def sum_middle(n, pair, factor):
+        arrived(PSR.at[n, pl.ds(0, 7)], pair[1])
+        total = PSS[n, f]
+        for j in range(1, 8):
+            total = total + PSR[n, fdev(j)]
+        PSG[n, f] = (total * factor).astype(bf16).astype(f32)
+        send, recv = send_id(), recv_id()
+        for j in range(1, 8):
+            go(PSG.at[n, f], send, recv, ctx, fdev(j))
+        return send, recv
+
+    def sum_end(n, pair):
+        arrived(PSG.at[n, pl.ds(0, 7)], pair[1])
+        return PSG[n].reshape(192, 128).astype(bf16)
+
     b_step(3)
-    x_relay(-2)
-    x_relay(2)
     a_step(1, 1)
+    a_step(1, 2)
+    x_relay(0)
+
+    below, above, across = fdev(6), fdev(2), fdev(4)
+    arrived(GB.at[below], g_low)
+    go(GB.at[below, half[0]], gs, g_low_half, ctx, above)
+    go(GB.at[below], gs, g_rest, ctx, partner)
+    arrived(GB.at[above], g_high)
+    go(GB.at[above, half[1]], gs, g_high_half, ctx, below)
+    go(GB.at[above], gs, g_rest, ctx, partner)
 
 
     @pl.when(is_host)
@@ -398,31 +417,47 @@
 
     arrived(PB(-4, 0), yb[-4])
     b_to_x(-4)
-    x_relay(-3)
-    x_relay(3)
     a_step(2, 0)
+    a_step(2, -1)
+    x_relay(-1)
+    x_relay(1)
+    arrived(AD2.at[pl.ds(0, 7)], ad2_r)
+    adapters = AD2[...].astype(f32).reshape(64, 1152).astype(bf16)
+    adapters = jnp.concatenate([adapters, jnp.zeros_like(adapters)], axis=0)
+    down_full, up_piece = adapters[:, :512], adapters[:, 512:]
+    back0 = sum_start(0, nt(GB[f], up_piece))
 
 
     @pl.when(is_host)
     def _():
         forward(2)
 
-    back0 = (back0, sum_middle(0, back0, adapter_scale))
-    x_relay(-4)
     a_step(2, 1)
+    a_step(2, 2)
+    x_relay(-2)
+    x_relay(2)
 
     @pl.when(is_host)
     def _():
         forward(3)
 
+    a_step(3, 0)
+    a_step(3, -1)
+    x_relay(-3)
+    x_relay(3)
+
+    back0 = (back0, sum_middle(0, back0, adapter_scale))
+    a_step(3, 1)
+    a_step(3, 2)
+
+    x_relay(-4)
     arrived(GB.at[across, half[0]], g_low_half)
     go(GB.at[across, half[0]], gs, g_rest, ctx, partner)
     arrived(GB.at[across, half[1]], g_high_half)
     go(GB.at[across, half[1]], gs, g_rest, ctx, partner)
 
-    a_step(3, 0)
-    a_step(3, 1)
-
+    arrived(OB, oi)
+    mid0 = sum_start(1, nt(OB[...], down_full))
     arrived(GB.at[pl.ds(0, 4)], g_rest)
 
     def a_part(d):
@@ -432,25 +467,27 @@
     total_a = a_part(0)
     for d in (-1, 1, -2, 2, -3, 3):
         total_a = total_a + a_part(d)
-    arrived(OB, oi)
-    mid0 = sum_start(1, nt(OB[...], down_full))
     lora_back = sum_end(0, back0[1])
     UPD[:, :, 0:512] = tn(lora_back, OB[...])[:64].reshape(8, 8, 512)
+    rs0_s, rs0_r = send_id(), recv_id()
+    for j in range(1, 8):
+        to = (g + j) % 8
+        go(UPD.at[to, :, 0:512], rs0_s, rs0_r, at(y, to), f, R1.at[g, :, 0:512])
     total_a = total_a + nn(lora_back, down_full[:, :256])
     total_b = nn(lora_back, down_full[:, 256:])
 
-
-    a_arrived(-4, 0)
-    a_arrived(4, 1)
-    total_a = total_a + a_part(4)
-    DOB[:, 0:256] = total_a.astype(bf16)
-    to_hosts(DOB, DU, di, ds, (0, 1))
 
     arrived(WB.at[pl.ds(0, 4)], xlast)
     for yy in range(8):
         total_b = total_b + nn(GB[yy], WB[yy].reshape(640, 256))
     DOB[:, 256:512] = total_b.astype(bf16)
     to_hosts(DOB, DU, di, ds, (2, 3))
+
+    for d, dx in ((-4, 0), (-4, -1), (4, 1), (4, 2)):
+        a_arrived(d, dx)
+    total_a = total_a + a_part(4)
+    DOB[:, 0:256] = total_a.astype(bf16)
+    to_hosts(DOB, DU, di, ds, (0, 1))
 
     gq, gk, gv = [recv_id() for _ in range(3)]
     hq, hk, hv = [send_id() for _ in range(3)]
@@ -495,34 +532,30 @@
     UPD[:, :, 512:1152] = (adapter_scale * tn(lora_mid, GB[f]))[:64].reshape(8, 8, 640)
     rs1_s, rs1_r = send_id(), recv_id()
     for j in range(1, 8):
-        go(UPD.at[row(j)], rs1_s, rs1_r, ydev(j), f, R1.at[y])
+        to = (g + j) % 8
+        go(UPD.at[to, :, 512:1152], rs1_s, rs1_r, at(y, to), f, R1.at[g, :, 512:1152])
 
 
     @pl.when(is_host)
     def _():
-        backward(2)
-
-    arrived(R1.at[pl.ds(0, 7)], rs1_r)
-    total = UPD[y]
+        for b in (2, 1, 0):
+            backward(b)
+
+    arrived(R1.at[pl.ds(0, 7), :, 0:512], rs0_r)
+    arrived(R1.at[pl.ds(0, 7), :, 512:1152], rs1_r)
+    total = UPD[g]
     for j in range(1, 8):
-        total = total + R1[row(j)]
+        total = total + R1[(g + j) % 8]
     for j in range(8):
         S2[j] = total[j : j + 1]
     rs2_s, rs2_r = send_id(), recv_id()
     for j in range(1, 8):
-        to = (g + j) % 8
-        go(S2.at[to], rs2_s, rs2_r, at(y, to), f, R2.at[g])
-
-
-    @pl.when(is_host)
-    def _():
-        for b in (1, 0):
-            backward(b)
+        go(S2.at[row(j)], rs2_s, rs2_r, ydev(j), f, R2.at[y])
 
     arrived(R2.at[pl.ds(0, 7)], rs2_r)
-    total = S2[g]
+    total = S2[y]
     for j in range(1, 8):
-        total = total + R2[(g + j) % 8]
+        total = total + R2[row(j)]
     dn_ref[...] = total[:, 0:512]
     up_ref[...] = total[:, 512:1152]
 
@@ -541,7 +574,8 @@
     left(PSG.at[0, seven], back0[1][0])
     left(PSS.at[1, seven], mid0[0])
     left(PSG.at[1, seven], mid1[0])
-    left(UPD.at[seven], rs1_s)
+    left(UPD.at[seven, :, 0:512], rs0_s)
+    left(UPD.at[seven, :, 512:1152], rs1_s)
     left(S2.at[seven], rs2_s)
 
     @pl.when(is_host)
@@ -560,8 +594,11 @@
 
 
 def finish_kernel(*refs):
-    for src, dst in zip(refs[:5], refs[5:]):
-        dst[...] = src[...]
+    copies = [pltpu.make_async_copy(refs[n], refs[5 + n], refs[10].at[n]) for n in range(5)]
+    for copy in copies:
+        copy.start()
+    for copy in copies:
+        copy.wait()
 
 
 def on_device(q, k, v, grad, codes, index, table, down, up):
@@ -579,7 +616,7 @@
             jax.ShapeDtypeStruct((1, width), f32),
             jax.ShapeDtypeStruct((1, grad.shape[1]), f32),
         ),
-        in_specs=[vmem] * 5 + [pl.BlockSpec(memory_space=pl.ANY)] * 4,
+        in_specs=[pl.BlockSpec(memory_space=pl.ANY)] * 9,
         out_specs=[vmem] * 5,
         scratch_shapes=[
             pltpu.VMEM((8, 8, 80, 256), bf16),
@@ -600,7 +637,7 @@
             pltpu.VMEM((1536, 128), f32),
             pltpu.VMEM((192, 512), bf16),
             pltpu.VMEM((8, 1, 1152), f32),
-            pltpu.VMEM((8, 8, 1152), f32),
+            pltpu.VMEM((8, 8, 1152), bf16),
             pltpu.VMEM((2, 8, 24, 128), f32),
             pltpu.VMEM((2, 8, 24, 128), f32),
             pltpu.VMEM((2, 8, 24, 128), f32),
@@ -608,9 +645,14 @@
             pltpu.VMEM((8, 8, 1152), f32),
             pltpu.VMEM((8, 1, 1152), f32),
             pltpu.VMEM((8, 1, 1152), f32),
+            pltpu.VMEM(codes.shape, jnp.int32),
+            pltpu.VMEM(index.shape[::-1], jnp.int32),
+            pltpu.VMEM((1, table.shape[0]), f32),
+            pltpu.VMEM(down.shape, bf16),
+            pltpu.VMEM(up.shape, bf16),
             pltpu.SemaphoreType.DMA((SENDS,)),
             pltpu.SemaphoreType.DMA((RECVS,)),
-            pltpu.SemaphoreType.DMA((1,)),
+            pltpu.SemaphoreType.DMA((6,)),
         ],
         compiler_params=pltpu.CompilerParams(
             collective_id=0, has_side_effects=True, vmem_limit_bytes=56 * 1024 * 1024
@@ -621,7 +663,8 @@
         name="finish",
         out_shape=tuple(jax.ShapeDtypeStruct(r.shape, r.dtype) for r in results),
         in_specs=[vmem] * 5,
-        out_specs=[vmem] * 5,
+        out_specs=[pl.BlockSpec(memory_space=pl.ANY)] * 5,
+        scratch_shapes=[pltpu.SemaphoreType.DMA((5,))],
     )(*results)
 
 

time: 98.2 us -> 84.9 us (0.86)
  the two profiles are of different devices: /device:TPU:1 before, /device:TPU:6 now
where the time goes in v4:
time: 84.9 us; the launch traced here: 84.7 us
  Pallas kernels  84.1 us (99%)
    pallas_call x1, Pallas kernels, on_device(): pl.pallas_call(kernel, name='block_backward', out_shape=(out, out, out, j...  82.1 us
    pallas_call x1, Pallas kernels, on_device(): pl.pallas_call(finish_kernel, name='finish', out_shape=tuple((jax.ShapeDt...  1.98 us

profile of v4, /device:TPU:6, one launch (start us, length us, event | category | flops | bytes accessed | tf_op | source)
XLA Modules:
  0.0 84.7 jit_solution(6214743221974724781)
XLA Ops:
  0.6 82.1 %block_backward.1 = (bf16[192,512]{1,0:T(8,128)(2,1)}, bf16[192,512]{1,0:T(8,128)(2,1)}, bf16[192,512]{1,0:T(8,128)(2,1)}, f32[1,512]{1,0:T(1,128)}, f32[1,640]{1,0:T(1,128)}) custom-call(s32[80,512]{1,0:T(8,128)} %codes_hbm.1, s32[8,80]{1,0:T(8,128)} %bitcast.2, f32[1,256]{1,0:T(1,128)} %bitcast.3, bf16[1,512]{1,0:T(2,128)(2,1)} %ad_hbm.1, ...), custom_call_target="tpu_custom_call" | custom-call | tf_op jit(solution)/shard_map/block_backward/pallas_call | solution.py:609
  82.7 2.0 %finish.1 = (bf16[192,512]{1,0:T(8,128)(2,1)}, bf16[192,512]{1,0:T(8,128)(2,1)}, bf16[192,512]{1,0:T(8,128)(2,1)}, f32[1,512]{1,0:T(1,128)}, f32[1,640]{1,0:T(1,128)}) custom-call(bf16[192,512]{1,0:T(8,128)(2,1)} %get-tuple-element.10.refs_0_, bf16[192,512]{1,0:T(8,128)(2,1)} %get-tuple-element.11.refs_1_, bf16[192,512]{1,0:T(8,128)(2,1)} %get-tuple-element.12.refs_2_, ...), custom_call_target="tpu_custom_call" | custom-call | tf_op jit(solution)/shard_map/finish/pallas_call | solution.py:661

commit v5 on v4

--- a/solution.py
+++ b/solution.py
@@ -48,7 +48,7 @@
     codes_hbm, index_hbm, table_hbm, ad_hbm, au_hbm, q_ref, k_ref, v_ref, g_ref,
     dq_ref, dk_ref, dv_ref, dn_ref, up_ref,
     WA, WB, GB, QU, KU, VU, DU, PT, KT, OB, OS, DQS, DKS, DVS, DKA, DVA, DOB,
-    AD1, AD2, PSS, PSR, PSG, UPD, R1, S2, R2, CODES, INDEX, TABLE, DOWN, UP, ss, rs, ls,
+    AD1, AD2, PS, UPD, R1, S2, R2, CODES, INDEX, TABLE, DOWN, UP, ss, rs, ls,
 ):
     ctx = lax.axis_index("ctx")
     f = lax.axis_index("fsdp")
@@ -369,27 +369,21 @@
             from_host(OS, OB, oh, oi, s)
 
     def sum_start(n, piece):
-        PSS[n] = piece.reshape(8, 24, 128)
+        PS[n, f] = piece.astype(bf16)
         send, recv = send_id(), recv_id()
         for j in range(1, 8):
-            to = fdev(j)
-            go(PSS.at[n, to], send, recv, ctx, to, PSR.at[n, f])
+            go(PS.at[n, f], send, recv, ctx, fdev(j))
         return send, recv
 
-    def sum_middle(n, pair, factor):
-        arrived(PSR.at[n, pl.ds(0, 7)], pair[1])
-        total = PSS[n, f]
+    def sum_end(n, pair, factor):
+        arrived(PS.at[n, pl.ds(0, 7)], pair[1])
+        total = PS[n, 0].astype(f32)
         for j in range(1, 8):
-            total = total + PSR[n, fdev(j)]
-        PSG[n, f] = (total * factor).astype(bf16).astype(f32)
-        send, recv = send_id(), recv_id()
-        for j in range(1, 8):
-            go(PSG.at[n, f], send, recv, ctx, fdev(j))
-        return send, recv
-
-    def sum_end(n, pair):
-        arrived(PSG.at[n, pl.ds(0, 7)], pair[1])
-        return PSG[n].reshape(192, 128).astype(bf16)
+            total = total + PS[n, j].astype(f32)
+        return (total * factor).astype(bf16)
+
+    def across_tokens(ranks, low, high):
+        return tn(ranks, low)[:64] + tn(ranks, high)[64:]
 
     b_step(3)
     a_step(1, 1)
@@ -412,7 +406,7 @@
         arrived(VU, vi)
         for kb in range(blocks):
             KT[:, kb * BLOCK : (kb + 1) * BLOCK] = two(KU, kb).astype(f32).T.astype(bf16)
-        for b in (0, 1):
+        for b in range(blocks):
             forward(b)
 
     arrived(PB(-4, 0), yb[-4])
@@ -423,41 +417,32 @@
     x_relay(1)
     arrived(AD2.at[pl.ds(0, 7)], ad2_r)
     adapters = AD2[...].astype(f32).reshape(64, 1152).astype(bf16)
-    adapters = jnp.concatenate([adapters, jnp.zeros_like(adapters)], axis=0)
-    down_full, up_piece = adapters[:, :512], adapters[:, 512:]
-    back0 = sum_start(0, nt(GB[f], up_piece))
-
-
-    @pl.when(is_host)
-    def _():
-        forward(2)
+    low = jnp.concatenate([adapters, jnp.zeros_like(adapters)], axis=0)
+    high = jnp.concatenate([jnp.zeros_like(adapters), adapters], axis=0)
+    down_low, up_low = low[:, :512], low[:, 512:]
+    down_high, up_high = high[:, :512], high[:, 512:]
+    back0 = sum_start(0, nt(GB[f, 0:96], up_low) + nt(GB[f, 96:192], up_high))
 
     a_step(2, 1)
     a_step(2, 2)
     x_relay(-2)
     x_relay(2)
-
-    @pl.when(is_host)
-    def _():
-        forward(3)
-
     a_step(3, 0)
     a_step(3, -1)
     x_relay(-3)
     x_relay(3)
 
-    back0 = (back0, sum_middle(0, back0, adapter_scale))
     a_step(3, 1)
     a_step(3, 2)
 
     x_relay(-4)
+    arrived(OB, oi)
+    mid0 = sum_start(1, nt(OB[0:96], down_low) + nt(OB[96:192], down_high))
     arrived(GB.at[across, half[0]], g_low_half)
     go(GB.at[across, half[0]], gs, g_rest, ctx, partner)
     arrived(GB.at[across, half[1]], g_high_half)
     go(GB.at[across, half[1]], gs, g_rest, ctx, partner)
 
-    arrived(OB, oi)
-    mid0 = sum_start(1, nt(OB[...], down_full))
     arrived(GB.at[pl.ds(0, 4)], g_rest)
 
     def a_part(d):
@@ -467,19 +452,14 @@
     total_a = a_part(0)
     for d in (-1, 1, -2, 2, -3, 3):
         total_a = total_a + a_part(d)
-    lora_back = sum_end(0, back0[1])
-    UPD[:, :, 0:512] = tn(lora_back, OB[...])[:64].reshape(8, 8, 512)
-    rs0_s, rs0_r = send_id(), recv_id()
-    for j in range(1, 8):
-        to = (g + j) % 8
-        go(UPD.at[to, :, 0:512], rs0_s, rs0_r, at(y, to), f, R1.at[g, :, 0:512])
-    total_a = total_a + nn(lora_back, down_full[:, :256])
-    total_b = nn(lora_back, down_full[:, 256:])
-
-
     arrived(WB.at[pl.ds(0, 4)], xlast)
-    for yy in range(8):
+    total_b = nn(GB[0], WB[0].reshape(640, 256))
+    for yy in range(1, 8):
         total_b = total_b + nn(GB[yy], WB[yy].reshape(640, 256))
+    lora_back = sum_end(0, back0, adapter_scale)
+    lora_term = jnp.concatenate([nn(lora_back, down_low), nn(lora_back, down_high)], axis=0)
+    total_a = total_a + lora_term[:, :256]
+    total_b = total_b + lora_term[:, 256:]
     DOB[:, 256:512] = total_b.astype(bf16)
     to_hosts(DOB, DU, di, ds, (2, 3))
 
@@ -521,25 +501,24 @@
         for s in (2 * b, 2 * b + 1):
             from_host(DQS, dq_ref, hq, gq, s)
 
-    mid1 = sum_middle(1, mid0, 1.0)
+    UPD[:, :, 0:512] = across_tokens(lora_back, OB[0:96], OB[96:192]).reshape(8, 8, 512)
+    rs0_s, rs0_r = send_id(), recv_id()
+    for j in range(1, 8):
+        to = (g + j) % 8
+        go(UPD.at[to, :, 0:512], rs0_s, rs0_r, at(y, to), f, R1.at[g, :, 0:512])
+    lora_mid = sum_end(1, mid0, adapter_scale)
+    up_part = across_tokens(lora_mid, GB[f, 0:96], GB[f, 96:192])
+    UPD[:, :, 512:1152] = up_part.reshape(8, 8, 640)
+    rs1_s, rs1_r = send_id(), recv_id()
+    for j in range(1, 8):
+        to = (g + j) % 8
+        go(UPD.at[to, :, 512:1152], rs1_s, rs1_r, at(y, to), f, R1.at[g, :, 512:1152])
+
 
     @pl.when(is_host)
     def _():
         arrived(DU, di)
         backward(3)
-
-    lora_mid = sum_end(1, mid1)
-    UPD[:, :, 512:1152] = (adapter_scale * tn(lora_mid, GB[f]))[:64].reshape(8, 8, 640)
-    rs1_s, rs1_r = send_id(), recv_id()
-    for j in range(1, 8):
-        to = (g + j) % 8
-        go(UPD.at[to, :, 512:1152], rs1_s, rs1_r, at(y, to), f, R1.at[g, :, 512:1152])
-
-
-    @pl.when(is_host)
-    def _():
-        for b in (2, 1, 0):
-            backward(b)
 
     arrived(R1.at[pl.ds(0, 7), :, 0:512], rs0_r)
     arrived(R1.at[pl.ds(0, 7), :, 512:1152], rs1_r)
@@ -552,6 +531,12 @@
     for j in range(1, 8):
         go(S2.at[row(j)], rs2_s, rs2_r, ydev(j), f, R2.at[y])
 
+
+    @pl.when(is_host)
+    def _():
+        for b in (2, 1, 0):
+            backward(b)
+
     arrived(R2.at[pl.ds(0, 7)], rs2_r)
     total = S2[y]
     for j in range(1, 8):
@@ -570,10 +555,8 @@
     left(GB.at[seven], gs)
     left(AD1.at[seven], ad1_s)
     left(AD2.at[seven], ad2_s)
-    left(PSS.at[0, seven], back0[0][0])
-    left(PSG.at[0, seven], back0[1][0])
-    left(PSS.at[1, seven], mid0[0])
-    left(PSG.at[1, seven], mid1[0])
+    left(PS.at[0, seven], back0[0])
+    left(PS.at[1, seven], mid0[0])
     left(UPD.at[seven, :, 0:512], rs0_s)
     left(UPD.at[seven, :, 512:1152], rs1_s)
     left(S2.at[seven], rs2_s)
@@ -638,9 +621,7 @@
             pltpu.VMEM((192, 512), bf16),
             pltpu.VMEM((8, 1, 1152), f32),
             pltpu.VMEM((8, 8, 1152), bf16),
-            pltpu.VMEM((2, 8, 24, 128), f32),
-            pltpu.VMEM((2, 8, 24, 128), f32),
-            pltpu.VMEM((2, 8, 24, 128), f32),
+            pltpu.VMEM((2, 8, 96, 128), bf16),
             pltpu.VMEM((8, 8, 1152), f32),
             pltpu.VMEM((8, 8, 1152), f32),
             pltpu.VMEM((8, 1, 1152), f32),

time: 84.9 us -> 81.9 us (0.965)
  the two profiles are of different devices: /device:TPU:6 before, /device:TPU:1 now
where the time goes in v5:
time: 81.9 us; the launch traced here: 81.8 us
  Pallas kernels  81.1 us (99%)
    pallas_call x1, Pallas kernels, on_device(): pl.pallas_call(kernel, name='block_backward', out_shape=(out, out, out, j...  79.2 us
    pallas_call x1, Pallas kernels, on_device(): pl.pallas_call(finish_kernel, name='finish', out_shape=tuple((jax.ShapeDt...  1.98 us

profile of v5, /device:TPU:1, one launch (start us, length us, event | category | flops | bytes accessed | tf_op | source)
XLA Modules:
  0.0 81.8 jit_solution(7732419398828928700)
XLA Ops:
  0.6 79.2 %block_backward.1 = (bf16[192,512]{1,0:T(8,128)(2,1)}, bf16[192,512]{1,0:T(8,128)(2,1)}, bf16[192,512]{1,0:T(8,128)(2,1)}, f32[1,512]{1,0:T(1,128)}, f32[1,640]{1,0:T(1,128)}) custom-call(s32[80,512]{1,0:T(8,128)} %codes_hbm.1, s32[8,80]{1,0:T(8,128)} %bitcast.2, f32[1,256]{1,0:T(1,128)} %bitcast.3, bf16[1,512]{1,0:T(2,128)(2,1)} %ad_hbm.1, ...), custom_call_target="tpu_custom_call" | custom-call | tf_op jit(solution)/shard_map/block_backward/pallas_call | solution.py:592
  79.8 2.0 %finish.1 = (bf16[192,512]{1,0:T(8,128)(2,1)}, bf16[192,512]{1,0:T(8,128)(2,1)}, bf16[192,512]{1,0:T(8,128)(2,1)}, f32[1,512]{1,0:T(1,128)}, f32[1,640]{1,0:T(1,128)}) custom-call(bf16[192,512]{1,0:T(8,128)(2,1)} %get-tuple-element.10.refs_0_, bf16[192,512]{1,0:T(8,128)(2,1)} %get-tuple-element.11.refs_1_, bf16[192,512]{1,0:T(8,128)(2,1)} %get-tuple-element.12.refs_2_, ...), custom_call_target="tpu_custom_call" | custom-call | tf_op jit(solution)/shard_map/finish/pallas_call | solution.py:642

commit v6 on v5

--- a/solution.py
+++ b/solution.py
@@ -29,7 +29,7 @@
 adapter_scale = 0.25
 masked = -1e30
 f32, bf16 = jnp.float32, jnp.bfloat16
-SENDS, RECVS = 24, 72
+SENDS, RECVS = 24, 76
 
 
 def nt(a, b):
@@ -261,12 +261,13 @@
 
     to_host_sends = []
 
-    def to_hosts(src_ref, dst_buf, recv, send, heads):
+    def to_hosts(src_ref, dst_buf, recvs, send, heads):
         for head in heads:
             dest = host_of(head)
             slot = slab_of(head)
             src = src_ref.at[:, head * 128 : (head + 1) * 128]
             dst = dst_buf.at[slot]
+            recv = recvs[0] + slot // 2 if len(recvs) > 1 else recvs[0]
             away = dest != ctx
 
             @pl.when(away)
@@ -277,13 +278,14 @@
             def _():
                 pltpu.make_async_copy(src, dst, rs.at[recv]).start()
 
-    ki, qi, vi, di = [recv_id() for _ in range(4)]
+    ki, qi, vi = [recv_id() for _ in range(3)]
+    di = [recv_id() for _ in range(4)]
     ks, qs, vs, ds = to_host_sends = [send_id() for _ in range(4)]
 
     def slabs():
-        to_hosts(k_ref, KU, ki, ks, range(4))
-        to_hosts(q_ref, QU, qi, qs, range(4))
-        to_hosts(v_ref, VU, vi, vs, range(4))
+        to_hosts(k_ref, KU, [ki], ks, range(4))
+        to_hosts(q_ref, QU, [qi], qs, range(4))
+        to_hosts(v_ref, VU, [vi], vs, range(4))
 
     for dx in (-1, 1):
         arrived(QA(0, dx), xa[dx])
@@ -432,17 +434,17 @@
     x_relay(-3)
     x_relay(3)
 
-    a_step(3, 1)
-    a_step(3, 2)
-
-    x_relay(-4)
-    arrived(OB, oi)
-    mid0 = sum_start(1, nt(OB[0:96], down_low) + nt(OB[96:192], down_high))
     arrived(GB.at[across, half[0]], g_low_half)
     go(GB.at[across, half[0]], gs, g_rest, ctx, partner)
     arrived(GB.at[across, half[1]], g_high_half)
     go(GB.at[across, half[1]], gs, g_rest, ctx, partner)
 
+    a_step(3, 1)
+    a_step(3, 2)
+
+    x_relay(-4)
+    arrived(OB, oi)
+    mid0 = sum_start(1, nt(OB[0:96], down_low) + nt(OB[96:192], down_high))
     arrived(GB.at[pl.ds(0, 4)], g_rest)
 
     def a_part(d):
@@ -473,6 +475,7 @@
     hq, hk, hv = [send_id() for _ in range(3)]
 
     def backward(b):
+        arrived(DU.at[pl.ds(2 * b, 2)], di[b])
         grad, query = two(DU, b), two(QU, b)
         parts = []
         delta = jnp.zeros((1, BLOCK), f32)
@@ -517,7 +520,6 @@
 
     @pl.when(is_host)
     def _():
-        arrived(DU, di)
         backward(3)
 
     arrived(R1.at[pl.ds(0, 7), :, 0:512], rs0_r)

time: 81.9 us -> 81.8 us (level)
  no operation moved by 1% of the time
where the time goes in v6:
time: 81.8 us; the launch traced here: 81.6 us
  Pallas kernels  81 us (99%)
    pallas_call x1, Pallas kernels, on_device(): pl.pallas_call(kernel, name='block_backward', out_shape=(out, out, out, j...  79 us
    pallas_call x1, Pallas kernels, on_device(): pl.pallas_call(finish_kernel, name='finish', out_shape=tuple((jax.ShapeDt...  1.98 us

profile of v6, /device:TPU:1, one launch (start us, length us, event | category | flops | bytes accessed | tf_op | source)
XLA Modules:
  0.0 81.6 jit_solution(4977501507048995573)
XLA Ops:
  0.6 79.0 %block_backward.1 = (bf16[192,512]{1,0:T(8,128)(2,1)}, bf16[192,512]{1,0:T(8,128)(2,1)}, bf16[192,512]{1,0:T(8,128)(2,1)}, f32[1,512]{1,0:T(1,128)}, f32[1,640]{1,0:T(1,128)}) custom-call(s32[80,512]{1,0:T(8,128)} %codes_hbm.1, s32[8,80]{1,0:T(8,128)} %bitcast.2, f32[1,256]{1,0:T(1,128)} %bitcast.3, bf16[1,512]{1,0:T(2,128)(2,1)} %ad_hbm.1, ...), custom_call_target="tpu_custom_call" | custom-call | tf_op jit(solution)/shard_map/block_backward/pallas_call | solution.py:594
  79.7 2.0 %finish.1 = (bf16[192,512]{1,0:T(8,128)(2,1)}, bf16[192,512]{1,0:T(8,128)(2,1)}, bf16[192,512]{1,0:T(8,128)(2,1)}, f32[1,512]{1,0:T(1,128)}, f32[1,640]{1,0:T(1,128)}) custom-call(bf16[192,512]{1,0:T(8,128)(2,1)} %get-tuple-element.10.refs_0_, bf16[192,512]{1,0:T(8,128)(2,1)} %get-tuple-element.11.refs_1_, bf16[192,512]{1,0:T(8,128)(2,1)} %get-tuple-element.12.refs_2_, ...), custom_call_target="tpu_custom_call" | custom-call | tf_op jit(solution)/shard_map/finish/pallas_call | solution.py:644
